TPU v7x, 32 devices: a whole 2x2x4 slice. The times are simulated.
32 devices in a mesh: row: 4 (over y, x), col: 8 (over z, core).
Axes of the slice: x: 2, y: 2, z: 4, core: 2. Of those that a mesh axis runs over, the one named last changes fastest.
Arguments:
- velocities: bfloat16 [1024, 30720], P(None, 'row'), may hold values from -60 to 60, as said below
- modes_panel: bfloat16 [30720, 4096], P('row', 'col'), may hold values from -1 to 1
- atom_slot: int32 [10240], P('row'), may hold values from 0 to 2559, as said below
- lag_offsets: int32 [8], replicated, may hold values from 0 to 256, as said below
Outputs:
- correlations: float32 [8, 4096, 4096], P(None, 'row', 'col')
Inputs may be any that keep to these rules, and one draw needn't show every extreme that they name: `velocities`: every snapshot row has its own scale. Within each aligned block of 2560 atoms, atom_slot is a permutation of 0 to 2559. `lag_offsets`: one of the lags equals 256.
All inputs are finite; a program needn't handle non-finite values.
Results may differ from a plain program's by a relative error of at most 0.0041.
Values may be sent and summed in bfloat16 or wider, within the bound.
No kernel may reach another device: no remote copies, remote signals or barrier semaphores. Data moves between devices by JAX's collectives and lax.ppermute only.
A program may use at most 128 MiB of HBM per device.

v0:
```python
import functools

import jax
import jax.numpy as jnp
from jax import lax
from jax.experimental import pallas as pl
from jax.experimental.pallas import tpu as pltpu
from jax.sharding import PartitionSpec as P


MAXLAG = 256
LANES = 128
ROWS = 8
GROUP = 16
TERMS = 3
MARGIN = 3 << 20
STEPS = 2

epsilon = 1e-06


def swap(block, axis, offset):
    size = lax.axis_size(axis)
    return lax.ppermute(block, axis, [(i, i ^ offset) for i in range(size)])


def reorder_chunk(slot, source, ordered, chunk, c):
    blocks = source.shape[0]
    row = lax.broadcasted_iota(jnp.int32, (ROWS, LANES), 0)
    groups = chunk // (3 * GROUP)

    def move(g, carry):
        g = c * groups + g
        base = [slot[g * GROUP + i] for i in range(GROUP)]
        for j in range(blocks):
            tiles = []
            for v in range(3 * GROUP // ROWS):
                tile = None
                for i in range(GROUP):
                    low = 3 * i - ROWS * v
                    if low + 3 <= 0 or low >= ROWS:
                        continue
                    piece = source[j, pl.ds(base[i] + (ROWS - low), ROWS), :]
                    tile = piece if tile is None else jnp.where(row >= low, piece, tile)
                tiles.append(tile)
            ordered[
                pl.ds(pl.multiple_of(g * 3 * GROUP, GROUP), 3 * GROUP), j * LANES : (j + 1) * LANES
            ] = jnp.concatenate(tiles, axis=0).astype(jnp.bfloat16)
        return carry

    lax.fori_loop(0, groups, move, 0, unroll=2)


def arrangement(lists):
    left, right = lists
    order = [m for m in left if m not in right] + [m for m in left if m in right]
    order += [m for m in right if m not in left]
    runs = [(min(order.index(m) for m in held), len(held)) for held in lists]
    return order, runs


def row_starts(order, size):
    mine = lax.axis_index("row")
    return [pl.multiple_of((mine ^ m) * size, size) for m in order]


def add_products(total, rows, part, ordered, runs, size):
    half = ordered.shape[1] // 2
    for h, (first, count) in enumerate(runs):
        columns = slice(h * half, (h + 1) * half)
        total[: count * size, columns] += jnp.dot(
            rows[first * size : (first + count) * size, part],
            ordered[part, columns],
            preferred_element_type=jnp.float32,
        )


def write_turned(total, outs):
    half, size = outs[0].shape
    count = len(outs) // 2
    for h in range(2):
        for i in range(count):
            outs[h * count + i][...] = total[i * size : (i + 1) * size, h * half : (h + 1) * half].T


def reorder_project_kernel(slot, panel, velocities, *refs, chunk, block, order, runs):
    count = runs[0][1]
    outs, ordered_out = refs[: 2 * count], refs[2 * count]
    tripled, slots, staged, source, rows, total, slot_sem, in_sems, row_sems, out_sem = refs[2 * count + 1 :]
    depth, width = panel.shape
    blocks = width // LANES
    size = outs[0].shape[1]
    chunks, steps = depth // chunk, depth // block
    starts = row_starts(order, size)

    def panel_copy(c):
        part = pl.ds(c * chunk, chunk)
        return pltpu.make_async_copy(panel.at[part, :], staged.at[part, :], in_sems.at[c])

    def row_copy(i, c):
        part = pl.ds(pl.multiple_of(c * block, block), block)
        return pltpu.make_async_copy(
            velocities.at[pl.ds(starts[i], size), part],
            rows.at[pl.ds(i * size, size), part],
            row_sems.at[c, i],
        )

    def ordered_copy(c):
        part = pl.ds(pl.multiple_of(c * block, block), block)
        return pltpu.make_async_copy(staged.at[part, :], ordered_out.at[part, :], out_sem)

    first_copy = pltpu.make_async_copy(slot, tripled, slot_sem)
    first_copy.start()
    for c in range(chunks):
        panel_copy(c).start()
    first_copy.wait()
    tripled[...] = tripled[...] * 3
    slot_copy = pltpu.make_async_copy(tripled, slots, slot_sem)
    slot_copy.start()
    total[...] = jnp.zeros_like(total)
    for c in range(chunks):
        panel_copy(c).wait()

        def widen(i, carry):
            first = pl.multiple_of(c * chunk + i * LANES, LANES)
            for j in range(blocks):
                source[j, pl.ds(ROWS + first, LANES), :] = staged[
                    pl.ds(first, LANES), j * LANES : (j + 1) * LANES
                ].astype(jnp.float32)
            return carry

        lax.fori_loop(0, chunk // LANES, widen, 0)
        later = c - (chunks - steps)
        if later >= 0:
            for i in range(len(order)):
                row_copy(i, later).start()
    slot_copy.wait()

    def body(c, carry):
        reorder_chunk(slots, source, staged, block, c)
        ordered_copy(c).start()
        for i in range(len(order)):
            row_copy(i, c).wait()
        part = pl.ds(pl.multiple_of(c * block, block), block)
        add_products(total, rows, part, staged, runs, size)
        return carry

    lax.fori_loop(0, steps, body, 0)
    write_turned(total, outs)
    for c in range(steps):
        ordered_copy(c).wait()


def reorder_project(panel, velocities, slot, lists, size):
    depth, width = panel.shape
    order, runs = arrangement(lists)
    count = runs[0][1]
    chunk, block = depth // 5, depth // STEPS
    anywhere = pl.BlockSpec(memory_space=pl.ANY)
    part = jax.ShapeDtypeStruct((width // 2, size), jnp.float32)
    *parts, ordered = pl.pallas_call(
        functools.partial(reorder_project_kernel, chunk=chunk, block=block, order=order, runs=runs),
        out_shape=[part] * (2 * count) + [jax.ShapeDtypeStruct((depth, width), jnp.bfloat16)],
        grid=(1,),
        in_specs=[pl.BlockSpec(memory_space=pltpu.HBM)] * 3,
        out_specs=[pl.BlockSpec((width // 2, size), lambda i: (0, 0))] * (2 * count) + [anywhere],
        scratch_shapes=[
            pltpu.VMEM(slot.shape, jnp.int32),
            pltpu.SMEM(slot.shape, jnp.int32),
            pltpu.VMEM((depth, width), jnp.bfloat16),
            pltpu.VMEM((width // LANES, depth + 2 * ROWS, LANES), jnp.float32),
            pltpu.VMEM((len(order) * size, depth), jnp.bfloat16),
            pltpu.VMEM((count * size, width), jnp.float32),
            pltpu.SemaphoreType.DMA,
            pltpu.SemaphoreType.DMA((depth // chunk,)),
            pltpu.SemaphoreType.DMA((depth // block, len(order))),
            pltpu.SemaphoreType.DMA,
        ],
        cost_estimate=pl.CostEstimate(
            flops=2 * count * size * depth * width,
            bytes_accessed=2 * depth * (2 * width + count * size),
            transcendentals=0,
        ),
        compiler_params=pltpu.CompilerParams(
            vmem_limit_bytes=2 * depth * (3 * width + len(order) * size) + 4 * size * width * count * 3 + MARGIN
        ),
        name="reorder_project",
    )(*(pltpu.with_memory_space_constraint(x, pltpu.HBM) for x in (slot, panel, velocities)))
    return parts_by_piece(parts, order, runs), ordered


def parts_by_piece(parts, order, runs):
    return [
        {m: parts[h * count + i] for i, m in enumerate(order[first : first + count])}
        for h, (first, count) in enumerate(runs)
    ]


def project_kernel(panel, velocities, *refs, chunk, order, runs):
    count = runs[0][1]
    outs = refs[: 2 * count]
    staged, rows, total, sems = refs[2 * count :]
    depth = panel.shape[0]
    size = outs[0].shape[1]
    chunks = depth // chunk
    starts = row_starts(order, size)

    def copies(c):
        part = pl.ds(c * chunk, chunk)
        yield pltpu.make_async_copy(panel.at[part, :], staged.at[part, :], sems.at[c, len(order)])
        for i, start in enumerate(starts):
            yield pltpu.make_async_copy(
                velocities.at[pl.ds(start, size), part], rows.at[pl.ds(i * size, size), part], sems.at[c, i]
            )

    for c in range(chunks):
        for copy in copies(c):
            copy.start()
    total[...] = jnp.zeros_like(total)
    for c in range(chunks):
        for copy in copies(c):
            copy.wait()
        add_products(total, rows, slice(c * chunk, (c + 1) * chunk), staged, runs, size)
    write_turned(total, outs)


def project(ordered, velocities, lists, size):
    depth, width = ordered.shape
    order, runs = arrangement(lists)
    count = runs[0][1]
    chunk = depth // 10
    anywhere = pl.BlockSpec(memory_space=pl.ANY)
    parts = pl.pallas_call(
        functools.partial(project_kernel, chunk=chunk, order=order, runs=runs),
        out_shape=[jax.ShapeDtypeStruct((width // 2, size), jnp.float32)] * (2 * count),
        grid=(1,),
        in_specs=[anywhere, pl.BlockSpec(memory_space=pltpu.HBM)],
        out_specs=[pl.BlockSpec((width // 2, size), lambda i: (0, 0))] * (2 * count),
        scratch_shapes=[
            pltpu.VMEM((depth, width), jnp.bfloat16),
            pltpu.VMEM((len(order) * size, depth), jnp.bfloat16),
            pltpu.VMEM((count * size, width), jnp.float32),
            pltpu.SemaphoreType.DMA((depth // chunk, len(order) + 1)),
        ],
        cost_estimate=pl.CostEstimate(
            flops=2 * count * size * depth * width,
            bytes_accessed=2 * depth * (width + len(order) * size),
            transcendentals=0,
        ),
        compiler_params=pltpu.CompilerParams(
            vmem_limit_bytes=2 * depth * (width + len(order) * size) + 4 * size * width * count * 3 + MARGIN
        ),
        name="project",
    )(ordered, pltpu.with_memory_space_constraint(velocities, pltpu.HBM))
    return parts_by_piece(parts, order, runs)


def shift_kernel(offsets, *refs, parts):
    pieces, (out, source, scales) = refs[:parts], refs[parts:]
    blocks, length, _ = source.shape
    size = pieces[0].shape[1]
    snapshots = parts * size

    @pl.when(pl.program_id(0) == 0)
    def _():
        for j in range(blocks):
            columns = slice(j * LANES, (j + 1) * LANES)
            for m, piece in enumerate(pieces):
                start = pl.multiple_of((lax.axis_index("row") ^ m) * size, size)
                source[j, pl.ds(start, size), :] = piece[columns, :].astype(jnp.float32).T
            source[j, snapshots:, :] = jnp.zeros((length - snapshots, LANES), jnp.float32)
        for m, piece in enumerate(pieces):
            start = pl.multiple_of((lax.axis_index("row") ^ m) * size, size)
            terms = piece[blocks * LANES :, :].astype(jnp.float32)
            scale = sum(terms[t : t + 1, :] for t in range(TERMS))
            scales[pl.ds(start, size), :] = jnp.broadcast_to(scale, (LANES, size)).T

    offset = offsets[pl.program_id(0)]
    step = 128

    def body(i, carry):
        first = pl.multiple_of(i * step, step)
        for j in range(blocks):
            late = source[j, pl.ds(first + offset, step), :] * scales[pl.ds(first, step), :]
            out[0, pl.ds(first, step), j * LANES : (j + 1) * LANES] = late.astype(jnp.bfloat16)
        return carry

    lax.fori_loop(0, snapshots // step, body, 0)


def shifted_copies(pieces, lag_offsets):
    rows, size = pieces[0].shape
    width = rows - GROUP
    parts = len(pieces)
    snapshots = size * parts
    lags = lag_offsets.shape[0]
    whole = pl.BlockSpec((rows, size), lambda l, s: (0, 0))
    return pl.pallas_call(
        functools.partial(shift_kernel, parts=parts),
        out_shape=jax.ShapeDtypeStruct((lags, snapshots, width), jnp.bfloat16),
        grid_spec=pltpu.PrefetchScalarGridSpec(
            num_scalar_prefetch=1,
            grid=(lags,),
            in_specs=[whole] * parts,
            out_specs=pl.BlockSpec((1, snapshots, width), lambda l, s: (l, 0, 0)),
            scratch_shapes=[
                pltpu.VMEM((width // LANES, snapshots + MAXLAG + ROWS, LANES), jnp.float32),
                pltpu.VMEM((snapshots, LANES), jnp.float32),
            ],
        ),
        cost_estimate=pl.CostEstimate(
            flops=0, bytes_accessed=2 * snapshots * width * (lags + 1), transcendentals=0
        ),
        compiler_params=pltpu.CompilerParams(
            vmem_limit_bytes=4 * width * (snapshots + MAXLAG) + 8 * snapshots * width + MARGIN
        ),
        name="shift",
    )(lag_offsets, *pieces)


def correlate_kernel(factors, *refs, parts, owners, half):
    mine, others = refs[:parts], refs[parts : parts + owners - 1]
    shifted = refs[parts + owners - 1]
    out, turned, lagged, results, in_sems, lag_sems, out_sems = refs[-7:]
    lags = shifted.shape[0]
    modes, size = mine[0].shape
    row = lax.axis_index("row")
    member = lax.rem(lax.axis_index("col"), owners)
    copies = []
    for m in range(parts):
        place = pl.ds(pl.multiple_of((row ^ m) * size, size), size)
        for k in range(owners):
            piece = mine[m] if k == 0 else others[k - 1].at[m]
            copies.append(
                pltpu.make_async_copy(piece, turned.at[pl.ds(k * modes, modes), place], in_sems.at[m, k])
            )
    for copy in copies:
        copy.start()

    def lag_copy(l):
        return pltpu.make_async_copy(shifted.at[l], lagged.at[l], lag_sems.at[l])

    def out_copies(l):
        for k in range(owners):
            first = ((member ^ k) * 2 + half) * modes
            yield pltpu.make_async_copy(
                results.at[l, pl.ds(k * modes, modes), :],
                out.at[l, pl.ds(pl.multiple_of(first, modes), modes), :],
                out_sems.at[l, k],
            )

    for l in range(lags):
        lag_copy(l).start()
    for copy in copies:
        copy.wait()

    def body(l, carry):
        lag_copy(l).wait()
        product = jnp.dot(turned[...], lagged[l], preferred_element_type=jnp.float32)
        results[l] = product * factors[l]
        for copy in out_copies(l):
            copy.start()
        return carry

    lax.fori_loop(0, lags, body, 0)
    for l in range(lags):
        for copy in out_copies(l):
            copy.wait()


def correlate(mine, others, shifted, factors, half, out_shape, previous):
    modes, _ = mine[0].shape
    parts, owners = len(mine), len(others) + 1
    lags, snapshots, width = shifted.shape
    operands = [*mine, *others, shifted]
    aliases = {}
    if previous is not None:
        aliases = {len(operands) + 1: 0}
        operands.append(previous)
    anywhere = pl.BlockSpec(memory_space=pl.ANY)
    return pl.pallas_call(
        functools.partial(correlate_kernel, parts=parts, owners=owners, half=half),
        out_shape=jax.ShapeDtypeStruct(out_shape, jnp.float32),
        grid_spec=pltpu.PrefetchScalarGridSpec(
            num_scalar_prefetch=1,
            grid=(1,),
            in_specs=[anywhere] * len(operands),
            out_specs=anywhere,
            scratch_shapes=[
                pltpu.VMEM((owners * modes, snapshots), jnp.bfloat16),
                pltpu.VMEM((lags, snapshots, width), jnp.bfloat16),
                pltpu.VMEM((lags, owners * modes, width), jnp.float32),
                pltpu.SemaphoreType.DMA((parts, owners)),
                pltpu.SemaphoreType.DMA((lags,)),
                pltpu.SemaphoreType.DMA((lags, owners)),
            ],
        ),
        input_output_aliases=aliases,
        cost_estimate=pl.CostEstimate(
            flops=2 * lags * owners * modes * snapshots * width,
            bytes_accessed=lags * width * (2 * snapshots + 4 * owners * modes),
            transcendentals=0,
        ),
        compiler_params=pltpu.CompilerParams(
            vmem_limit_bytes=lags * width * (2 * snapshots + 4 * owners * modes)
            + 2 * owners * modes * snapshots
            + MARGIN
        ),
        name="correlate",
    )(factors, *operands)


def reduce_scatter(held, bits):
    live = range(len(held))
    held = dict(held)
    for bit in bits:
        for m in reversed(live):
            if m & bit:
                arrived = swap(held[m], "row", bit)
                held[m ^ bit] = held[m ^ bit] + arrived
        live = [m for m in live if not m & bit]
    return held[0]


def steps(velocities, modes_panel, atom_slot, lag_offsets):
    ranks = lax.axis_size("row")
    columns = lax.axis_size("col")
    owners = columns // ranks
    mine = lax.axis_index("row")
    group = lax.axis_index("col") // owners
    snapshots = velocities.shape[0]
    size = snapshots // ranks
    width = modes_panel.shape[1]
    modes = width * columns

    bits = [1 << b for b in range(ranks.bit_length() - 1)]
    orders = [bits, bits[::-1]]
    early = [[m for m in range(ranks) if m & order[0]] for order in orders]
    late = [[m for m in range(ranks) if not m & order[0]] for order in orders]
    early_parts, ordered = reorder_project(modes_panel, velocities, atom_slot, early, size)
    late_parts = project(ordered, velocities, late, size)
    halves = [reduce_scatter(early_parts[h] | late_parts[h], orders[h]) for h in range(2)]

    raw = [half.astype(jnp.bfloat16) for half in halves]
    across = []
    for h in range(2):
        across.append([raw[h]] + [swap(raw[h], "col", owners * m) for m in range(1, ranks)])

    energy = sum(jnp.sum(half * half, axis=0) for half in halves)
    steps_left = columns.bit_length() - 1
    for step in [*range(1, steps_left), 0]:
        arrived = swap(energy, "col", 1 << step)
        energy = energy + arrived
    scale = lax.rsqrt(energy / modes + epsilon)[None, :]
    own = [(half * scale).astype(jnp.bfloat16) for half in halves]
    rest = scale
    for _ in range(TERMS):
        term = lax.reduce_precision(rest, 8, 7)
        rest = rest - term
        own.append(term.astype(jnp.bfloat16))
    own.append(jnp.zeros((GROUP - TERMS, size), jnp.bfloat16))
    own = jnp.concatenate(own, axis=0)
    column_pieces = [own] + [swap(own, "row", m) for m in range(1, ranks)]
    shifted = shifted_copies(column_pieces, lag_offsets)

    factors = lax.rsqrt((snapshots - lag_offsets).astype(jnp.float32))
    out_shape = (lag_offsets.shape[0], width * owners, width)
    result = None
    for h in range(2):
        if h == 1:
            across[h], shifted = lax.optimization_barrier((across[h], shifted))
        stacked = jnp.stack(across[h])
        pieces = []
        for m in range(ranks):
            chosen = lax.dynamic_index_in_dim(stacked, group ^ mine ^ m, 0, keepdims=False)
            if m:
                chosen = swap(chosen, "row", m)
            pieces.append(chosen)
        if h == 1:
            pieces, result = lax.optimization_barrier((pieces, result))
        joined = jnp.stack(pieces)
        others = [swap(joined, "col", k) for k in range(1, owners)]
        result = correlate(pieces, others, shifted, factors, h, out_shape, result)
    return result


def solution(mesh):
    return jax.shard_map(
        steps,
        mesh=mesh,
        in_specs=(P(None, "row"), P("row", "col"), P("row"), P()),
        out_specs=P(None, "row", "col"),
        check_vma=False,
    )
```

profile of v0, /device:TPU:0, one launch (start us, length us, event | category | flops | bytes accessed | tf_op | source)
XLA Modules:
  0.0 119.2 jit_solution(2303388626372747537)
XLA Ops:
  0.0 14.6 %reorder_project.1 = (f32[256,256]{1,0:T(8,128)S(1)}, f32[256,256]{1,0:T(8,128)S(1)}, f32[256,256]{1,0:T(8,128)S(1)}, f32[256,256]{1,0:T(8,128)S(1)}, bf16[7680,512]{1,0:T(8,128)(2,1)S(1)}) custom-call(s32[2560]{0:T(1024)} %slot.1, bf16[7680,512]{1,0:T(8,128)(2,1)} %panel.1, bf16[1024,7680]{1,0:T(8,128)(2,1)} %velocities.3), custom_call_target="tpu_custom_call" | custom-call | flops 4026531840 | bytes 23592960 | tf_op jit(solution)/shard_map/reorder_project/pallas_call | solution.py:161
  14.6 3.0 %collective-permute-start.1 = (f32[256,256]{1,0:T(8,128)S(1)}, f32[256,256]{1,0:T(8,128)S(1)}, u32[]{:S(2)}, u32[]{:S(2)}) collective-permute-start(f32[256,256]{1,0:T(8,128)S(1)} %get-tuple-element.28), channel_id=1, source_target_pairs={{0,16},{8,24},{16,0},{24,8},{1,17},{9,25},{17,1},{25,9},{2,18},{10... | collective-permute-start | bytes 786440 | tf_op jit(solution)/shard_map/ppermute | solution.py:24
  17.6 1.5 %collective-permute-start.6 = (f32[256,256]{1,0:T(8,128)S(1)}, f32[256,256]{1,0:T(8,128)S(1)}, u32[]{:S(2)}, u32[]{:S(2)}) collective-permute-start(f32[256,256]{1,0:T(8,128)S(1)} %get-tuple-element.30), channel_id=1, source_target_pairs={{0,8},{8,0},{16,24},{24,16},{1,9},{9,1},{17,25},{25,17},{2,10},{10... | collective-permute-start | bytes 786440 | tf_op jit(solution)/shard_map/ppermute | solution.py:24
  19.1 0.5 collective-permute-start.7
  19.6 6.6 %project.1 = (f32[256,256]{1,0:T(8,128)S(1)}, f32[256,256]{1,0:T(8,128)S(1)}, f32[256,256]{1,0:T(8,128)S(1)}, f32[256,256]{1,0:T(8,128)S(1)}) custom-call(bf16[7680,512]{1,0:T(8,128)(2,1)S(1)} %get-tuple-element.24.panel, bf16[1024,7680]{1,0:T(8,128)(2,1)} %velocities.3), custom_call_target="tpu_custom_call" | custom-call | flops 4026531840 | bytes 19660800 | tf_op jit(solution)/shard_map/project/pallas_call | solution.py:233
  26.2 4.8 %collective-permute-done.7 = f32[256,256]{1,0:T(8,128)S(1)} collective-permute-done((f32[256,256]{1,0:T(8,128)S(1)}, f32[256,256]{1,0:T(8,128)S(1)}, u32[]{:S(2)}, u32[]{:S(2)}) %collective-permute-start.7) | collective-permute-done | bytes 262176 | tf_op jit(solution)/shard_map/ppermute | solution.py:24
  31.0 0.4 collective-permute-start.8
  31.4 1.7 %collective-permute-start = (f32[256,256]{1,0:T(8,128)S(1)}, f32[256,256]{1,0:T(8,128)S(1)}, u32[]{:S(2)}, u32[]{:S(2)}) collective-permute-start(f32[256,256]{1,0:T(8,128)S(1)} %get-tuple-element.26), channel_id=1, source_target_pairs={{0,16},{8,24},{16,0},{24,8},{1,17},{9,25},{17,1},{25,9},{2,18},{10... | collective-permute-start | bytes 786440 | tf_op jit(solution)/shard_map/ppermute | solution.py:24
  33.1 0.0 collective-permute-done.1
  33.2 1.6 %collective-permute-start.2 = (f32[256,256]{1,0:T(8,128)S(1)}, f32[256,256]{1,0:T(8,128)S(1)}, u32[]{:S(2)}, u32[]{:S(2)}) collective-permute-start(f32[256,256]{1,0:T(8,128)S(1)} %add.55), channel_id=1, source_target_pairs={{0,8},{8,0},{16,24},{24,16},{1,9},{9,1},{17,25},{25,17},{2,10},{10... | collective-permute-start | bytes 786440 | tf_op jit(solution)/shard_map/ppermute | solution.py:24
  34.7 0.0 collective-permute-done.6
  34.7 5.5 %collective-permute-done.8 = f32[256,256]{1,0:T(8,128)S(1)} collective-permute-done((f32[256,256]{1,0:T(8,128)S(1)}, f32[256,256]{1,0:T(8,128)S(1)}, u32[]{:S(2)}, u32[]{:S(2)}) %collective-permute-start.8) | collective-permute-done | bytes 262176 | tf_op jit(solution)/shard_map/ppermute | solution.py:24
  40.3 0.1 fusion.2
  40.3 0.1 multiply_reduce_fusion.1
  40.4 3.2 %collective-permute-done = f32[256,256]{1,0:T(8,128)S(1)} collective-permute-done((f32[256,256]{1,0:T(8,128)S(1)}, f32[256,256]{1,0:T(8,128)S(1)}, u32[]{:S(2)}, u32[]{:S(2)}) %collective-permute-start) | collective-permute-done | bytes 262176 | tf_op jit(solution)/shard_map/ppermute | solution.py:24
  43.6 0.0 collective-permute-done.2
  43.6 0.1 multiply_reduce_fusion
  43.7 1.6 %collective-permute-start.9 = (f32[256]{0:T(256)S(1)}, f32[256]{0:T(256)S(1)}, u32[]{:S(2)}, u32[]{:S(2)}) collective-permute-start(f32[256]{0:T(256)S(1)} %add.60), channel_id=1, source_target_pairs={{0,2},{1,3},{2,0},{3,1},{4,6},{5,7},{6,4},{7,5},{8,10},{9,11},{10,... | collective-permute-start | bytes 3080 | tf_op jit(solution)/shard_map/ppermute | solution.py:24
  45.3 2.0 %collective-permute-done.9 = f32[256]{0:T(256)S(1)} collective-permute-done((f32[256]{0:T(256)S(1)}, f32[256]{0:T(256)S(1)}, u32[]{:S(2)}, u32[]{:S(2)}) %collective-permute-start.9) | collective-permute-done | bytes 1056 | tf_op jit(solution)/shard_map/ppermute | solution.py:24
  47.3 2.6 %collective-permute-start.10 = (f32[256]{0:T(256)S(1)}, f32[256]{0:T(256)S(1)}, u32[]{:S(2)}, u32[]{:S(2)}) collective-permute-start(f32[256]{0:T(256)S(1)} %add.61), channel_id=1, source_target_pairs={{0,4},{1,5},{2,6},{3,7},{4,0},{5,1},{6,2},{7,3},{8,12},{9,13},{10,... | collective-permute-start | bytes 3080 | tf_op jit(solution)/shard_map/ppermute | solution.py:24
  49.9 1.9 %collective-permute-done.10 = f32[256]{0:T(256)S(1)} collective-permute-done((f32[256]{0:T(256)S(1)}, f32[256]{0:T(256)S(1)}, u32[]{:S(2)}, u32[]{:S(2)}) %collective-permute-start.10) | collective-permute-done | bytes 1056 | tf_op jit(solution)/shard_map/ppermute | solution.py:24
  51.8 0.0 collective-permute-start.11
  51.8 3.6 %collective-permute-start.20 = (bf16[256,256]{1,0:T(8,128)(2,1)S(1)}, bf16[256,256]{1,0:T(8,128)(2,1)S(1)}, u32[]{:S(2)}, u32[]{:S(2)}) collective-permute-start(bf16[256,256]{1,0:T(8,128)(2,1)S(1)} %get-tuple-element.43), channel_id=1, source_target_pairs={{0,6},{1,7},{2,4},{3,5},{4,2},{5,3},{6,0},{7,1},{8,14},{9,15},{10,... | collective-permute-start | bytes 393224 | tf_op jit(solution)/shard_map/ppermute | solution.py:24
  55.4 0.0 collective-permute-start.19
  55.4 0.8 collective-permute-start.18
  56.2 0.0 collective-permute-done.11
  56.2 0.1 multiply_convert_fusion
  56.3 3.8 %collective-permute-done.20 = bf16[256,256]{1,0:T(8,128)(2,1)S(1)} collective-permute-done((bf16[256,256]{1,0:T(8,128)(2,1)S(1)}, bf16[256,256]{1,0:T(8,128)(2,1)S(1)}, u32[]{:S(2)}, u32[]{:S(2)}) %collective-permute-start.20) | collective-permute-done | bytes 131104 | tf_op jit(solution)/shard_map/ppermute | solution.py:24
  60.1 7.1 %collective-permute-done.19 = bf16[256,256]{1,0:T(8,128)(2,1)S(1)} collective-permute-done((bf16[256,256]{1,0:T(8,128)(2,1)S(1)}, bf16[256,256]{1,0:T(8,128)(2,1)S(1)}, u32[]{:S(2)}, u32[]{:S(2)}) %collective-permute-start.19) | collective-permute-done | bytes 131104 | tf_op jit(solution)/shard_map/ppermute | solution.py:24
  67.2 0.0 collective-permute-done.18
  67.2 0.1 pad_maximum_fusion.1
  67.3 1.5 %collective-permute-start.23 = (bf16[256,256]{1,0:T(8,128)(2,1)S(1)}, bf16[256,256]{1,0:T(8,128)(2,1)S(1)}, u32[]{:S(2)}, u32[]{:S(2)}) collective-permute-start(bf16[256,256]{1,0:T(8,128)(2,1)S(1)} %get-tuple-element.49), channel_id=1, source_target_pairs={{0,24},{8,16},{16,8},{24,0},{1,25},{9,17},{17,9},{25,1},{2,26},{10... | collective-permute-start | bytes 393224 | tf_op jit(solution)/shard_map/ppermute | solution.py:24
  68.8 1.5 %collective-permute-start.22 = (bf16[256,256]{1,0:T(8,128)(2,1)S(1)}, bf16[256,256]{1,0:T(8,128)(2,1)S(1)}, u32[]{:S(2)}, u32[]{:S(2)}) collective-permute-start(bf16[256,256]{1,0:T(8,128)(2,1)S(1)} %get-tuple-element.50), channel_id=1, source_target_pairs={{0,16},{8,24},{16,0},{24,8},{1,17},{9,25},{17,1},{25,9},{2,18},{10... | collective-permute-start | bytes 393224 | tf_op jit(solution)/shard_map/ppermute | solution.py:24
  70.3 0.5 collective-permute-start.21
  70.9 0.2 concatenate.3.refs_0_
  71.1 1.5 %collective-permute-start.14 = (bf16[528,256]{1,0:T(8,128)(2,1)S(1)}, bf16[528,256]{1,0:T(8,128)(2,1)S(1)}, u32[]{:S(2)}, u32[]{:S(2)}) collective-permute-start(bf16[528,256]{1,0:T(8,128)(2,1)S(1)} %concatenate.3.refs_0_), channel_id=1, source_target_pairs={{0,24},{8,16},{16,8},{24,0},{1,25},{9,17},{17,9},{25,1},{2,26},{10... | collective-permute-start | bytes 811016 | tf_op jit(solution)/shard_map/ppermute | solution.py:24
  72.6 1.5 %collective-permute-start.13 = (bf16[528,256]{1,0:T(8,128)(2,1)S(1)}, bf16[528,256]{1,0:T(8,128)(2,1)S(1)}, u32[]{:S(2)}, u32[]{:S(2)}) collective-permute-start(bf16[528,256]{1,0:T(8,128)(2,1)S(1)} %concatenate.3.refs_0_), channel_id=1, source_target_pairs={{0,16},{8,24},{16,0},{24,8},{1,17},{9,25},{17,1},{25,9},{2,18},{10... | collective-permute-start | bytes 811016 | tf_op jit(solution)/shard_map/ppermute | solution.py:24
  74.1 0.5 collective-permute-done.23.refs_3_
  74.6 7.5 %collective-permute-done.22.refs_2_ = bf16[256,256]{1,0:T(8,128)(2,1)S(1)} collective-permute-done((bf16[256,256]{1,0:T(8,128)(2,1)S(1)}, bf16[256,256]{1,0:T(8,128)(2,1)S(1)}, u32[]{:S(2)}, u32[]{:S(2)}) %collective-permute-start.22) | collective-permute-done | bytes 131104 | tf_op jit(solution)/shard_map/ppermute | solution.py:24
  82.1 0.0 collective-permute-done.21.refs_1_
  82.1 0.1 pad_maximum_fusion.2
  82.2 0.1 collective-permute-start.24
  82.3 1.5 %collective-permute-start.12 = (bf16[528,256]{1,0:T(8,128)(2,1)S(1)}, bf16[528,256]{1,0:T(8,128)(2,1)S(1)}, u32[]{:S(2)}, u32[]{:S(2)}) collective-permute-start(bf16[528,256]{1,0:T(8,128)(2,1)S(1)} %concatenate.3.refs_0_), channel_id=1, source_target_pairs={{0,8},{8,0},{16,24},{24,16},{1,9},{9,1},{17,25},{25,17},{2,10},{10... | collective-permute-start | bytes 811016 | tf_op jit(solution)/shard_map/ppermute | solution.py:24
  83.7 2.5 %collective-permute-start.5 = (bf16[256,256]{1,0:T(8,128)(2,1)S(1)}, bf16[256,256]{1,0:T(8,128)(2,1)S(1)}, u32[]{:S(2)}, u32[]{:S(2)}) collective-permute-start(bf16[256,256]{1,0:T(8,128)(2,1)S(1)} %get-tuple-element.33), channel_id=1, source_target_pairs={{0,6},{1,7},{2,4},{3,5},{4,2},{5,3},{6,0},{7,1},{8,14},{9,15},{10,... | collective-permute-start | bytes 393224 | tf_op jit(solution)/shard_map/ppermute | solution.py:24
  86.2 0.0 collective-permute-done.14.refs_3_
  86.2 0.0 collective-permute-start.4
  86.2 1.5 %collective-permute-done.13.refs_2_ = bf16[528,256]{1,0:T(8,128)(2,1)S(1)} collective-permute-done((bf16[528,256]{1,0:T(8,128)(2,1)S(1)}, bf16[528,256]{1,0:T(8,128)(2,1)S(1)}, u32[]{:S(2)}, u32[]{:S(2)}) %collective-permute-start.13) | collective-permute-done | bytes 270368 | tf_op jit(solution)/shard_map/ppermute | solution.py:24
  87.7 0.4 collective-permute-start.3
  88.1 3.0 %collective-permute-done.12.refs_1_ = bf16[528,256]{1,0:T(8,128)(2,1)S(1)} collective-permute-done((bf16[528,256]{1,0:T(8,128)(2,1)S(1)}, bf16[528,256]{1,0:T(8,128)(2,1)S(1)}, u32[]{:S(2)}, u32[]{:S(2)}) %collective-permute-start.12) | collective-permute-done | bytes 270368 | tf_op jit(solution)/shard_map/ppermute | solution.py:24
  91.1 2.8 %shift.1.refs_5_ = bf16[8,1024,512]{2,1,0:T(8,128)(2,1)S(1)} custom-call(s32[8]{0:T(128)S(1)} %copy-done, bf16[528,256]{1,0:T(8,128)(2,1)S(1)} %concatenate.3.refs_0_, bf16[528,256]{1,0:T(8,128)(2,1)S(1)} %collective-permute-done.12.refs_1_, bf16[528,256]{1,0:T(8,128)(2,1)S(1)} %collective-permute-done.13.refs_2_, ...), custom_call_target="tpu_custom_call" | custom-call | bytes 9437184 | tf_op jit(solution)/shard_map/shift/pallas_call | solution.py:298
  94.0 0.0 collective-permute-done.5
  94.0 3.0 %collective-permute-done.4 = bf16[256,256]{1,0:T(8,128)(2,1)S(1)} collective-permute-done((bf16[256,256]{1,0:T(8,128)(2,1)S(1)}, bf16[256,256]{1,0:T(8,128)(2,1)S(1)}, u32[]{:S(2)}, u32[]{:S(2)}) %collective-permute-start.4) | collective-permute-done | bytes 131104 | tf_op jit(solution)/shard_map/ppermute | solution.py:24
  97.0 0.1 pad_maximum_fusion
  97.1 0.8 collective-permute-start.17
  97.9 1.4 %collective-permute-start.16 = (bf16[256,256]{1,0:T(8,128)(2,1)S(1)}, bf16[256,256]{1,0:T(8,128)(2,1)S(1)}, u32[]{:S(2)}, u32[]{:S(2)}) collective-permute-start(bf16[256,256]{1,0:T(8,128)(2,1)S(1)} %get-tuple-element.54), channel_id=1, source_target_pairs={{0,16},{8,24},{16,0},{24,8},{1,17},{9,25},{17,1},{25,9},{2,18},{10... | collective-permute-start | bytes 393224 | tf_op jit(solution)/shard_map/ppermute | solution.py:24
  99.3 1.4 %collective-permute-start.15 = (bf16[256,256]{1,0:T(8,128)(2,1)S(1)}, bf16[256,256]{1,0:T(8,128)(2,1)S(1)}, u32[]{:S(2)}, u32[]{:S(2)}) collective-permute-start(bf16[256,256]{1,0:T(8,128)(2,1)S(1)} %get-tuple-element.55), channel_id=1, source_target_pairs={{0,8},{8,0},{16,24},{24,16},{1,9},{9,1},{17,25},{25,17},{2,10},{10... | collective-permute-start | bytes 393224 | tf_op jit(solution)/shard_map/ppermute | solution.py:24
  100.7 0.0 collective-permute-done.24.refs_4_
  100.7 8.2 %correlate.2.refs_6_ = f32[8,1024,512]{2,1,0:T(8,128)} custom-call(f32[8]{0:T(128)S(1)} %convert_rsqrt_fusion.factors, bf16[256,256]{1,0:T(8,128)(2,1)S(1)} %bitcast.30, bf16[256,256]{1,0:T(8,128)(2,1)S(1)} %collective-permute-done.21.refs_1_, bf16[256,256]{1,0:T(8,128)(2,1)S(1)} %collective-permute-done.22.refs_2_, ...), custom_call_target="tpu_custom_call" | custom-call | flops 4294967296 | bytes 16777216 | tf_op jit(solution)/shard_map/correlate/pallas_call | solution.py:381
  108.9 0.0 collective-permute-done.16.refs_2_
  108.9 0.0 collective-permute-done.15.refs_1_
  108.9 0.1 pad_maximum_fusion.3
  109.0 0.1 collective-permute-start.25
  109.1 1.9 %collective-permute-done.25.refs_4_ = bf16[4,256,256]{2,1,0:T(8,128)(2,1)S(1)} collective-permute-done((bf16[4,256,256]{2,1,0:T(8,128)(2,1)S(1)}, bf16[4,256,256]{2,1,0:T(8,128)(2,1)S(1)}, u32[]{:S(2)}, u32[]{:S(2)}) %collective-permute-start.25) | collective-permute-done | bytes 524320 | tf_op jit(solution)/shard_map/ppermute | solution.py:24
  111.0 8.2 %correlate.3 = f32[8,1024,512]{2,1,0:T(8,128)} custom-call(f32[8]{0:T(128)S(1)} %convert_rsqrt_fusion.factors, bf16[256,256]{1,0:T(8,128)(2,1)S(1)} %get-tuple-element.37.refs_0_, bf16[256,256]{1,0:T(8,128)(2,1)S(1)} %collective-permute-done.15.refs_1_, bf16[256,256]{1,0:T(8,128)(2,1)S(1)} %collective-permute-done.16.refs_2_, ...), custom_call_target="tpu_custom_call", output_to_operand_aliasing={{}: (7, {})} | custom-call | flops 4294967296 | bytes 16777216 | tf_op jit(solution)/shard_map/correlate/pallas_call | solution.py:381
  (18 shorter events, 0.2 us)
Async XLA Ops:
  14.6 18.5 %collective-permute-start.1 = (f32[256,256]{1,0:T(8,128)S(1)}, f32[256,256]{1,0:T(8,128)S(1)}, u32[]{:S(2)}, u32[]{:S(2)}) collective-permute-start(f32[256,256]{1,0:T(8,128)S(1)} %get-tuple-element.28), channel_id=1, source_target_pairs={{0,16},{8,24},{16,0},{24,8},{1,17},{9,25},{17,1},{25,9},{2,18},{10... | collective-permute-start | bytes 786440 | tf_op jit(solution)/shard_map/ppermute | solution.py:24
  17.6 17.1 %collective-permute-start.6 = (f32[256,256]{1,0:T(8,128)S(1)}, f32[256,256]{1,0:T(8,128)S(1)}, u32[]{:S(2)}, u32[]{:S(2)}) collective-permute-start(f32[256,256]{1,0:T(8,128)S(1)} %get-tuple-element.30), channel_id=1, source_target_pairs={{0,8},{8,0},{16,24},{24,16},{1,9},{9,1},{17,25},{25,17},{2,10},{10... | collective-permute-start | bytes 786440 | tf_op jit(solution)/shard_map/ppermute | solution.py:24
  19.1 11.9 %collective-permute-start.7 = (f32[256,256]{1,0:T(8,128)S(1)}, f32[256,256]{1,0:T(8,128)S(1)}, u32[]{:S(2)}, u32[]{:S(2)}) collective-permute-start(f32[256,256]{1,0:T(8,128)S(1)} %get-tuple-element.32), channel_id=1, source_target_pairs={{0,8},{8,0},{16,24},{24,16},{1,9},{9,1},{17,25},{25,17},{2,10},{10... | collective-permute-start | bytes 786440 | tf_op jit(solution)/shard_map/ppermute | solution.py:24
  19.6 68.5 %copy-start = (s32[8]{0:T(128)S(1)}, s32[8]{0:T(128)}, u32[]{:S(2)}) copy-start(s32[8]{0:T(128)} %offsets.1) | copy-start | bytes 100
  31.0 9.2 %collective-permute-start.8 = (f32[256,256]{1,0:T(8,128)S(1)}, f32[256,256]{1,0:T(8,128)S(1)}, u32[]{:S(2)}, u32[]{:S(2)}) collective-permute-start(f32[256,256]{1,0:T(8,128)S(1)} %add.58), channel_id=1, source_target_pairs={{0,16},{8,24},{16,0},{24,8},{1,17},{9,25},{17,1},{25,9},{2,18},{10... | collective-permute-start | bytes 786440 | tf_op jit(solution)/shard_map/ppermute | solution.py:24
  31.4 12.2 %collective-permute-start = (f32[256,256]{1,0:T(8,128)S(1)}, f32[256,256]{1,0:T(8,128)S(1)}, u32[]{:S(2)}, u32[]{:S(2)}) collective-permute-start(f32[256,256]{1,0:T(8,128)S(1)} %get-tuple-element.26), channel_id=1, source_target_pairs={{0,16},{8,24},{16,0},{24,8},{1,17},{9,25},{17,1},{25,9},{2,18},{10... | collective-permute-start | bytes 786440 | tf_op jit(solution)/shard_map/ppermute | solution.py:24
  33.2 10.5 %collective-permute-start.2 = (f32[256,256]{1,0:T(8,128)S(1)}, f32[256,256]{1,0:T(8,128)S(1)}, u32[]{:S(2)}, u32[]{:S(2)}) collective-permute-start(f32[256,256]{1,0:T(8,128)S(1)} %add.55), channel_id=1, source_target_pairs={{0,8},{8,0},{16,24},{24,16},{1,9},{9,1},{17,25},{25,17},{2,10},{10... | collective-permute-start | bytes 786440 | tf_op jit(solution)/shard_map/ppermute | solution.py:24
  43.7 3.6 %collective-permute-start.9 = (f32[256]{0:T(256)S(1)}, f32[256]{0:T(256)S(1)}, u32[]{:S(2)}, u32[]{:S(2)}) collective-permute-start(f32[256]{0:T(256)S(1)} %add.60), channel_id=1, source_target_pairs={{0,2},{1,3},{2,0},{3,1},{4,6},{5,7},{6,4},{7,5},{8,10},{9,11},{10,... | collective-permute-start | bytes 3080 | tf_op jit(solution)/shard_map/ppermute | solution.py:24
  47.3 4.5 %collective-permute-start.10 = (f32[256]{0:T(256)S(1)}, f32[256]{0:T(256)S(1)}, u32[]{:S(2)}, u32[]{:S(2)}) collective-permute-start(f32[256]{0:T(256)S(1)} %add.61), channel_id=1, source_target_pairs={{0,4},{1,5},{2,6},{3,7},{4,0},{5,1},{6,2},{7,3},{8,12},{9,13},{10,... | collective-permute-start | bytes 3080 | tf_op jit(solution)/shard_map/ppermute | solution.py:24
  51.8 4.4 %collective-permute-start.11 = (f32[256]{0:T(256)S(1)}, f32[256]{0:T(256)S(1)}, u32[]{:S(2)}, u32[]{:S(2)}) collective-permute-start(f32[256]{0:T(256)S(1)} %add.62), channel_id=1, source_target_pairs={{0,1},{1,0},{2,3},{3,2},{4,5},{5,4},{6,7},{7,6},{8,9},{9,8},{10,11... | collective-permute-start | bytes 3080 | tf_op jit(solution)/shard_map/ppermute | solution.py:24
  51.8 8.3 %collective-permute-start.20 = (bf16[256,256]{1,0:T(8,128)(2,1)S(1)}, bf16[256,256]{1,0:T(8,128)(2,1)S(1)}, u32[]{:S(2)}, u32[]{:S(2)}) collective-permute-start(bf16[256,256]{1,0:T(8,128)(2,1)S(1)} %get-tuple-element.43), channel_id=1, source_target_pairs={{0,6},{1,7},{2,4},{3,5},{4,2},{5,3},{6,0},{7,1},{8,14},{9,15},{10,... | collective-permute-start | bytes 393224 | tf_op jit(solution)/shard_map/ppermute | solution.py:24
  55.4 11.7 %collective-permute-start.19 = (bf16[256,256]{1,0:T(8,128)(2,1)S(1)}, bf16[256,256]{1,0:T(8,128)(2,1)S(1)}, u32[]{:S(2)}, u32[]{:S(2)}) collective-permute-start(bf16[256,256]{1,0:T(8,128)(2,1)S(1)} %get-tuple-element.43), channel_id=1, source_target_pairs={{0,4},{1,5},{2,6},{3,7},{4,0},{5,1},{6,2},{7,3},{8,12},{9,13},{10,... | collective-permute-start | bytes 393224 | tf_op jit(solution)/shard_map/ppermute | solution.py:24
  55.4 11.7 %collective-permute-start.18 = (bf16[256,256]{1,0:T(8,128)(2,1)S(1)}, bf16[256,256]{1,0:T(8,128)(2,1)S(1)}, u32[]{:S(2)}, u32[]{:S(2)}) collective-permute-start(bf16[256,256]{1,0:T(8,128)(2,1)S(1)} %get-tuple-element.43), channel_id=1, source_target_pairs={{0,2},{1,3},{2,0},{3,1},{4,6},{5,7},{6,4},{7,5},{8,10},{9,11},{10,... | collective-permute-start | bytes 393224 | tf_op jit(solution)/shard_map/ppermute | solution.py:24
  67.3 7.3 %collective-permute-start.23 = (bf16[256,256]{1,0:T(8,128)(2,1)S(1)}, bf16[256,256]{1,0:T(8,128)(2,1)S(1)}, u32[]{:S(2)}, u32[]{:S(2)}) collective-permute-start(bf16[256,256]{1,0:T(8,128)(2,1)S(1)} %get-tuple-element.49), channel_id=1, source_target_pairs={{0,24},{8,16},{16,8},{24,0},{1,25},{9,17},{17,9},{25,1},{2,26},{10... | collective-permute-start | bytes 393224 | tf_op jit(solution)/shard_map/ppermute | solution.py:24
  68.8 13.3 %collective-permute-start.22 = (bf16[256,256]{1,0:T(8,128)(2,1)S(1)}, bf16[256,256]{1,0:T(8,128)(2,1)S(1)}, u32[]{:S(2)}, u32[]{:S(2)}) collective-permute-start(bf16[256,256]{1,0:T(8,128)(2,1)S(1)} %get-tuple-element.50), channel_id=1, source_target_pairs={{0,16},{8,24},{16,0},{24,8},{1,17},{9,25},{17,1},{25,9},{2,18},{10... | collective-permute-start | bytes 393224 | tf_op jit(solution)/shard_map/ppermute | solution.py:24
  70.3 11.8 %collective-permute-start.21 = (bf16[256,256]{1,0:T(8,128)(2,1)S(1)}, bf16[256,256]{1,0:T(8,128)(2,1)S(1)}, u32[]{:S(2)}, u32[]{:S(2)}) collective-permute-start(bf16[256,256]{1,0:T(8,128)(2,1)S(1)} %get-tuple-element.51), channel_id=1, source_target_pairs={{0,8},{8,0},{16,24},{24,16},{1,9},{9,1},{17,25},{25,17},{2,10},{10... | collective-permute-start | bytes 393224 | tf_op jit(solution)/shard_map/ppermute | solution.py:24
  71.1 15.2 %collective-permute-start.14 = (bf16[528,256]{1,0:T(8,128)(2,1)S(1)}, bf16[528,256]{1,0:T(8,128)(2,1)S(1)}, u32[]{:S(2)}, u32[]{:S(2)}) collective-permute-start(bf16[528,256]{1,0:T(8,128)(2,1)S(1)} %concatenate.3.refs_0_), channel_id=1, source_target_pairs={{0,24},{8,16},{16,8},{24,0},{1,25},{9,17},{17,9},{25,1},{2,26},{10... | collective-permute-start | bytes 811016 | tf_op jit(solution)/shard_map/ppermute | solution.py:24
  72.6 15.1 %collective-permute-start.13 = (bf16[528,256]{1,0:T(8,128)(2,1)S(1)}, bf16[528,256]{1,0:T(8,128)(2,1)S(1)}, u32[]{:S(2)}, u32[]{:S(2)}) collective-permute-start(bf16[528,256]{1,0:T(8,128)(2,1)S(1)} %concatenate.3.refs_0_), channel_id=1, source_target_pairs={{0,16},{8,24},{16,0},{24,8},{1,17},{9,25},{17,1},{25,9},{2,18},{10... | collective-permute-start | bytes 811016 | tf_op jit(solution)/shard_map/ppermute | solution.py:24
  82.2 18.5 %collective-permute-start.24 = (bf16[4,256,256]{2,1,0:T(8,128)(2,1)S(1)}, bf16[4,256,256]{2,1,0:T(8,128)(2,1)S(1)}, u32[]{:S(2)}, u32[]{:S(2)}) collective-permute-start(bf16[4,256,256]{2,1,0:T(8,128)(2,1)S(1)} %pad_maximum_fusion.2), channel_id=1, source_target_pairs={{0,1},{1,0},{2,3},{3,2},{4,5},{5,4},{6,7},{7,6},{8,9},{9,8},{10,11... | collective-permute-start | bytes 1572872 | tf_op jit(solution)/shard_map/ppermute | solution.py:24
  82.3 8.9 %collective-permute-start.12 = (bf16[528,256]{1,0:T(8,128)(2,1)S(1)}, bf16[528,256]{1,0:T(8,128)(2,1)S(1)}, u32[]{:S(2)}, u32[]{:S(2)}) collective-permute-start(bf16[528,256]{1,0:T(8,128)(2,1)S(1)} %concatenate.3.refs_0_), channel_id=1, source_target_pairs={{0,8},{8,0},{16,24},{24,16},{1,9},{9,1},{17,25},{25,17},{2,10},{10... | collective-permute-start | bytes 811016 | tf_op jit(solution)/shard_map/ppermute | solution.py:24
  83.7 10.3 %collective-permute-start.5 = (bf16[256,256]{1,0:T(8,128)(2,1)S(1)}, bf16[256,256]{1,0:T(8,128)(2,1)S(1)}, u32[]{:S(2)}, u32[]{:S(2)}) collective-permute-start(bf16[256,256]{1,0:T(8,128)(2,1)S(1)} %get-tuple-element.33), channel_id=1, source_target_pairs={{0,6},{1,7},{2,4},{3,5},{4,2},{5,3},{6,0},{7,1},{8,14},{9,15},{10,... | collective-permute-start | bytes 393224 | tf_op jit(solution)/shard_map/ppermute | solution.py:24
  86.2 10.8 %collective-permute-start.4 = (bf16[256,256]{1,0:T(8,128)(2,1)S(1)}, bf16[256,256]{1,0:T(8,128)(2,1)S(1)}, u32[]{:S(2)}, u32[]{:S(2)}) collective-permute-start(bf16[256,256]{1,0:T(8,128)(2,1)S(1)} %get-tuple-element.33), channel_id=1, source_target_pairs={{0,4},{1,5},{2,6},{3,7},{4,0},{5,1},{6,2},{7,3},{8,12},{9,13},{10,... | collective-permute-start | bytes 393224 | tf_op jit(solution)/shard_map/ppermute | solution.py:24
  87.7 9.3 %collective-permute-start.3 = (bf16[256,256]{1,0:T(8,128)(2,1)S(1)}, bf16[256,256]{1,0:T(8,128)(2,1)S(1)}, u32[]{:S(2)}, u32[]{:S(2)}) collective-permute-start(bf16[256,256]{1,0:T(8,128)(2,1)S(1)} %get-tuple-element.33), channel_id=1, source_target_pairs={{0,2},{1,3},{2,0},{3,1},{4,6},{5,7},{6,4},{7,5},{8,10},{9,11},{10,... | collective-permute-start | bytes 393224 | tf_op jit(solution)/shard_map/ppermute | solution.py:24
  97.1 11.8 %collective-permute-start.17 = (bf16[256,256]{1,0:T(8,128)(2,1)S(1)}, bf16[256,256]{1,0:T(8,128)(2,1)S(1)}, u32[]{:S(2)}, u32[]{:S(2)}) collective-permute-start(bf16[256,256]{1,0:T(8,128)(2,1)S(1)} %get-tuple-element.53), channel_id=1, source_target_pairs={{0,24},{8,16},{16,8},{24,0},{1,25},{9,17},{17,9},{25,1},{2,26},{10... | collective-permute-start | bytes 393224 | tf_op jit(solution)/shard_map/ppermute | solution.py:24
  97.9 11.0 %collective-permute-start.16 = (bf16[256,256]{1,0:T(8,128)(2,1)S(1)}, bf16[256,256]{1,0:T(8,128)(2,1)S(1)}, u32[]{:S(2)}, u32[]{:S(2)}) collective-permute-start(bf16[256,256]{1,0:T(8,128)(2,1)S(1)} %get-tuple-element.54), channel_id=1, source_target_pairs={{0,16},{8,24},{16,0},{24,8},{1,17},{9,25},{17,1},{25,9},{2,18},{10... | collective-permute-start | bytes 393224 | tf_op jit(solution)/shard_map/ppermute | solution.py:24
  99.3 9.6 %collective-permute-start.15 = (bf16[256,256]{1,0:T(8,128)(2,1)S(1)}, bf16[256,256]{1,0:T(8,128)(2,1)S(1)}, u32[]{:S(2)}, u32[]{:S(2)}) collective-permute-start(bf16[256,256]{1,0:T(8,128)(2,1)S(1)} %get-tuple-element.55), channel_id=1, source_target_pairs={{0,8},{8,0},{16,24},{24,16},{1,9},{9,1},{17,25},{25,17},{2,10},{10... | collective-permute-start | bytes 393224 | tf_op jit(solution)/shard_map/ppermute | solution.py:24
  109.0 2.0 %collective-permute-start.25 = (bf16[4,256,256]{2,1,0:T(8,128)(2,1)S(1)}, bf16[4,256,256]{2,1,0:T(8,128)(2,1)S(1)}, u32[]{:S(2)}, u32[]{:S(2)}) collective-permute-start(bf16[4,256,256]{2,1,0:T(8,128)(2,1)S(1)} %pad_maximum_fusion.3), channel_id=1, source_target_pairs={{0,1},{1,0},{2,3},{3,2},{4,5},{5,4},{6,7},{7,6},{8,9},{9,8},{10,11... | collective-permute-start | bytes 1572872 | tf_op jit(solution)/shard_map/ppermute | solution.py:24
where the time goes:
time: 119 us
  waiting for transfers between devices  45.7 us (38%)
  Pallas kernels  40.4 us (34%)
  starting transfers between devices  32 us (27%)
    ppermute x26, waiting for transfers between devices, swap(): return lax.ppermute(block, axis, [(i, i ^ offset) for i in range(size)])  45.7 us
    ppermute x26, starting transfers between devices, swap(): return lax.ppermute(block, axis, [(i, i ^ offset) for i in range(size)])  32 us
    pallas_call x2, Pallas kernels, correlate(): pl.pallas_call(functools.partial(correlate_kernel, parts=parts, owners=ow...  16.4 us
    pallas_call x1, Pallas kernels, reorder_project(): pl.pallas_call(functools.partial(reorder_project_kernel, chunk=chunk, blo...  14.6 us
    pallas_call x1, Pallas kernels, project(): pl.pallas_call(functools.partial(project_kernel, chunk=chunk, order=order...  6.57 us
    pallas_call x1, Pallas kernels, shifted_copies(): pl.pallas_call(functools.partial(shift_kernel, parts=parts), out_shape=ja...  2.85 us
  transfers between devices with their start and end apart: 26, of which 13 were waited for; matrix products, arithmetic and copies ran while one was open for 1% of the time, Pallas kernels for 15%

commit v1 on v0

--- a/solution.py
+++ b/solution.py
@@ -85,8 +85,8 @@
 
 def reorder_project_kernel(slot, panel, velocities, *refs, chunk, block, order, runs):
     count = runs[0][1]
-    outs, ordered_out = refs[: 2 * count], refs[2 * count]
-    tripled, slots, staged, source, rows, total, slot_sem, in_sems, row_sems, out_sem = refs[2 * count + 1 :]
+    outs, ordered = refs[: 2 * count], refs[2 * count]
+    tripled, slots, staged, source, rows, total, slot_sem, in_sems, row_sems = refs[2 * count + 1 :]
     depth, width = panel.shape
     blocks = width // LANES
     size = outs[0].shape[1]
@@ -104,10 +104,6 @@
             rows.at[pl.ds(i * size, size), part],
             row_sems.at[c, i],
         )
-
-    def ordered_copy(c):
-        part = pl.ds(pl.multiple_of(c * block, block), block)
-        return pltpu.make_async_copy(staged.at[part, :], ordered_out.at[part, :], out_sem)
 
     first_copy = pltpu.make_async_copy(slot, tripled, slot_sem)
     first_copy.start()
@@ -137,18 +133,15 @@
     slot_copy.wait()
 
     def body(c, carry):
-        reorder_chunk(slots, source, staged, block, c)
-        ordered_copy(c).start()
+        reorder_chunk(slots, source, ordered, block, c)
         for i in range(len(order)):
             row_copy(i, c).wait()
         part = pl.ds(pl.multiple_of(c * block, block), block)
-        add_products(total, rows, part, staged, runs, size)
+        add_products(total, rows, part, ordered, runs, size)
         return carry
 
     lax.fori_loop(0, steps, body, 0)
     write_turned(total, outs)
-    for c in range(steps):
-        ordered_copy(c).wait()
 
 
 def reorder_project(panel, velocities, slot, lists, size):
@@ -156,14 +149,12 @@
     order, runs = arrangement(lists)
     count = runs[0][1]
     chunk, block = depth // 5, depth // STEPS
-    anywhere = pl.BlockSpec(memory_space=pl.ANY)
     part = jax.ShapeDtypeStruct((width // 2, size), jnp.float32)
     *parts, ordered = pl.pallas_call(
         functools.partial(reorder_project_kernel, chunk=chunk, block=block, order=order, runs=runs),
         out_shape=[part] * (2 * count) + [jax.ShapeDtypeStruct((depth, width), jnp.bfloat16)],
-        grid=(1,),
         in_specs=[pl.BlockSpec(memory_space=pltpu.HBM)] * 3,
-        out_specs=[pl.BlockSpec((width // 2, size), lambda i: (0, 0))] * (2 * count) + [anywhere],
+        out_specs=[pl.BlockSpec(memory_space=pltpu.VMEM)] * (2 * count + 1),
         scratch_shapes=[
             pltpu.VMEM(slot.shape, jnp.int32),
             pltpu.SMEM(slot.shape, jnp.int32),
@@ -174,7 +165,6 @@
             pltpu.SemaphoreType.DMA,
             pltpu.SemaphoreType.DMA((depth // chunk,)),
             pltpu.SemaphoreType.DMA((depth // block, len(order))),
-            pltpu.SemaphoreType.DMA,
         ],
         cost_estimate=pl.CostEstimate(
             flops=2 * count * size * depth * width,
@@ -199,7 +189,7 @@
 def project_kernel(panel, velocities, *refs, chunk, order, runs):
     count = runs[0][1]
     outs = refs[: 2 * count]
-    staged, rows, total, sems = refs[2 * count :]
+    rows, total, sems = refs[2 * count :]
     depth = panel.shape[0]
     size = outs[0].shape[1]
     chunks = depth // chunk
@@ -207,7 +197,6 @@
 
     def copies(c):
         part = pl.ds(c * chunk, chunk)
-        yield pltpu.make_async_copy(panel.at[part, :], staged.at[part, :], sems.at[c, len(order)])
         for i, start in enumerate(starts):
             yield pltpu.make_async_copy(
                 velocities.at[pl.ds(start, size), part], rows.at[pl.ds(i * size, size), part], sems.at[c, i]
@@ -220,7 +209,7 @@
     for c in range(chunks):
         for copy in copies(c):
             copy.wait()
-        add_products(total, rows, slice(c * chunk, (c + 1) * chunk), staged, runs, size)
+        add_products(total, rows, slice(c * chunk, (c + 1) * chunk), panel, runs, size)
     write_turned(total, outs)
 
 
@@ -229,18 +218,15 @@
     order, runs = arrangement(lists)
     count = runs[0][1]
     chunk = depth // 10
-    anywhere = pl.BlockSpec(memory_space=pl.ANY)
     parts = pl.pallas_call(
         functools.partial(project_kernel, chunk=chunk, order=order, runs=runs),
         out_shape=[jax.ShapeDtypeStruct((width // 2, size), jnp.float32)] * (2 * count),
-        grid=(1,),
-        in_specs=[anywhere, pl.BlockSpec(memory_space=pltpu.HBM)],
-        out_specs=[pl.BlockSpec((width // 2, size), lambda i: (0, 0))] * (2 * count),
+        in_specs=[pl.BlockSpec(memory_space=pltpu.VMEM), pl.BlockSpec(memory_space=pltpu.HBM)],
+        out_specs=[pl.BlockSpec(memory_space=pltpu.VMEM)] * (2 * count),
         scratch_shapes=[
-            pltpu.VMEM((depth, width), jnp.bfloat16),
             pltpu.VMEM((len(order) * size, depth), jnp.bfloat16),
             pltpu.VMEM((count * size, width), jnp.float32),
-            pltpu.SemaphoreType.DMA((depth // chunk, len(order) + 1)),
+            pltpu.SemaphoreType.DMA((depth // chunk, len(order))),
         ],
         cost_estimate=pl.CostEstimate(
             flops=2 * count * size * depth * width,
@@ -248,7 +234,7 @@
             transcendentals=0,
         ),
         compiler_params=pltpu.CompilerParams(
-            vmem_limit_bytes=2 * depth * (width + len(order) * size) + 4 * size * width * count * 3 + MARGIN
+            vmem_limit_bytes=2 * depth * len(order) * size + 4 * size * width * count * 3 + MARGIN
         ),
         name="project",
     )(ordered, pltpu.with_memory_space_constraint(velocities, pltpu.HBM))
@@ -321,7 +307,7 @@
 def correlate_kernel(factors, *refs, parts, owners, half):
     mine, others = refs[:parts], refs[parts : parts + owners - 1]
     shifted = refs[parts + owners - 1]
-    out, turned, lagged, results, in_sems, lag_sems, out_sems = refs[-7:]
+    out, turned, results, in_sems, out_sems = refs[-5:]
     lags = shifted.shape[0]
     modes, size = mine[0].shape
     row = lax.axis_index("row")
@@ -337,9 +323,6 @@
     for copy in copies:
         copy.start()
 
-    def lag_copy(l):
-        return pltpu.make_async_copy(shifted.at[l], lagged.at[l], lag_sems.at[l])
-
     def out_copies(l):
         for k in range(owners):
             first = ((member ^ k) * 2 + half) * modes
@@ -349,14 +332,11 @@
                 out_sems.at[l, k],
             )
 
-    for l in range(lags):
-        lag_copy(l).start()
     for copy in copies:
         copy.wait()
 
     def body(l, carry):
-        lag_copy(l).wait()
-        product = jnp.dot(turned[...], lagged[l], preferred_element_type=jnp.float32)
+        product = jnp.dot(turned[...], shifted[l], preferred_element_type=jnp.float32)
         results[l] = product * factors[l]
         for copy in out_copies(l):
             copy.start()
@@ -372,29 +352,26 @@
     modes, _ = mine[0].shape
     parts, owners = len(mine), len(others) + 1
     lags, snapshots, width = shifted.shape
+    anywhere = pl.BlockSpec(memory_space=pl.ANY)
     operands = [*mine, *others, shifted]
+    in_specs = [pl.BlockSpec(memory_space=pltpu.SMEM)] + [anywhere] * (len(operands) - 1)
+    in_specs.append(pl.BlockSpec(memory_space=pltpu.VMEM))
     aliases = {}
     if previous is not None:
         aliases = {len(operands) + 1: 0}
         operands.append(previous)
-    anywhere = pl.BlockSpec(memory_space=pl.ANY)
+        in_specs.append(anywhere)
     return pl.pallas_call(
         functools.partial(correlate_kernel, parts=parts, owners=owners, half=half),
         out_shape=jax.ShapeDtypeStruct(out_shape, jnp.float32),
-        grid_spec=pltpu.PrefetchScalarGridSpec(
-            num_scalar_prefetch=1,
-            grid=(1,),
-            in_specs=[anywhere] * len(operands),
-            out_specs=anywhere,
-            scratch_shapes=[
-                pltpu.VMEM((owners * modes, snapshots), jnp.bfloat16),
-                pltpu.VMEM((lags, snapshots, width), jnp.bfloat16),
-                pltpu.VMEM((lags, owners * modes, width), jnp.float32),
-                pltpu.SemaphoreType.DMA((parts, owners)),
-                pltpu.SemaphoreType.DMA((lags,)),
-                pltpu.SemaphoreType.DMA((lags, owners)),
-            ],
-        ),
+        in_specs=in_specs,
+        out_specs=anywhere,
+        scratch_shapes=[
+            pltpu.VMEM((owners * modes, snapshots), jnp.bfloat16),
+            pltpu.VMEM((lags, owners * modes, width), jnp.float32),
+            pltpu.SemaphoreType.DMA((parts, owners)),
+            pltpu.SemaphoreType.DMA((lags, owners)),
+        ],
         input_output_aliases=aliases,
         cost_estimate=pl.CostEstimate(
             flops=2 * lags * owners * modes * snapshots * width,
@@ -402,7 +379,7 @@
             transcendentals=0,
         ),
         compiler_params=pltpu.CompilerParams(
-            vmem_limit_bytes=lags * width * (2 * snapshots + 4 * owners * modes)
+            vmem_limit_bytes=lags * width * 4 * owners * modes
             + 2 * owners * modes * snapshots
             + MARGIN
         ),

time: 119 us -> 118 us (level)
  Pallas kernels: 40.4 us -> 38.5 us
  transfers between devices with their start and end apart: 26 -> 26, of which waited for: 13 -> 13; matrix products, arithmetic and copies ran while one was open for 1% -> 1% of each run, Pallas kernels for 15% -> 14%
where the time goes in v1:
time: 118 us; the launch traced here: 117 us
  waiting for transfers between devices  45.9 us (39%)
  Pallas kernels  38.5 us (33%)
  starting transfers between devices  32 us (27%)
    ppermute x26, waiting for transfers between devices, swap(): return lax.ppermute(block, axis, [(i, i ^ offset) for i in range(size)])  45.9 us
    ppermute x26, starting transfers between devices, swap(): return lax.ppermute(block, axis, [(i, i ^ offset) for i in range(size)])  32 us
    pallas_call x2, Pallas kernels, correlate(): pl.pallas_call(functools.partial(correlate_kernel, parts=parts, owners=ow...  15.2 us
    pallas_call x1, Pallas kernels, reorder_project(): pl.pallas_call(functools.partial(reorder_project_kernel, chunk=chunk, blo...  14 us
    pallas_call x1, Pallas kernels, project(): pl.pallas_call(functools.partial(project_kernel, chunk=chunk, order=order...  6.43 us
    pallas_call x1, Pallas kernels, shifted_copies(): pl.pallas_call(functools.partial(shift_kernel, parts=parts), out_shape=ja...  2.85 us
  transfers between devices with their start and end apart: 26, of which 13 were waited for; matrix products, arithmetic and copies ran while one was open for 1% of the time, Pallas kernels for 14%

profile of v1, /device:TPU:0, one launch (start us, length us, event | category | flops | bytes accessed | tf_op | source)
XLA Modules:
  0.0 117.5 jit_solution(9038161772293779576)
XLA Ops:
  0.0 14.0 %reorder_project.1 = (f32[256,256]{1,0:T(8,128)S(1)}, f32[256,256]{1,0:T(8,128)S(1)}, f32[256,256]{1,0:T(8,128)S(1)}, f32[256,256]{1,0:T(8,128)S(1)}, bf16[7680,512]{1,0:T(8,128)(2,1)S(1)}) custom-call(s32[2560]{0:T(1024)} %slot.1, bf16[7680,512]{1,0:T(8,128)(2,1)} %panel.1, bf16[1024,7680]{1,0:T(8,128)(2,1)} %velocities.3), custom_call_target="tpu_custom_call" | custom-call | flops 4026531840 | bytes 23592960 | tf_op jit(solution)/shard_map/reorder_project/pallas_call | solution.py:153
  14.0 3.0 %collective-permute-start.1 = (f32[256,256]{1,0:T(8,128)S(1)}, f32[256,256]{1,0:T(8,128)S(1)}, u32[]{:S(2)}, u32[]{:S(2)}) collective-permute-start(f32[256,256]{1,0:T(8,128)S(1)} %get-tuple-element.28), channel_id=1, source_target_pairs={{0,16},{8,24},{16,0},{24,8},{1,17},{9,25},{17,1},{25,9},{2,18},{10... | collective-permute-start | bytes 786440 | tf_op jit(solution)/shard_map/ppermute | solution.py:24
  17.0 1.5 %collective-permute-start.6 = (f32[256,256]{1,0:T(8,128)S(1)}, f32[256,256]{1,0:T(8,128)S(1)}, u32[]{:S(2)}, u32[]{:S(2)}) collective-permute-start(f32[256,256]{1,0:T(8,128)S(1)} %get-tuple-element.30), channel_id=1, source_target_pairs={{0,8},{8,0},{16,24},{24,16},{1,9},{9,1},{17,25},{25,17},{2,10},{10... | collective-permute-start | bytes 786440 | tf_op jit(solution)/shard_map/ppermute | solution.py:24
  18.5 0.5 collective-permute-start.7
  19.0 6.4 %project.1 = (f32[256,256]{1,0:T(8,128)S(1)}, f32[256,256]{1,0:T(8,128)S(1)}, f32[256,256]{1,0:T(8,128)S(1)}, f32[256,256]{1,0:T(8,128)S(1)}) custom-call(bf16[7680,512]{1,0:T(8,128)(2,1)S(1)} %get-tuple-element.24.panel, bf16[1024,7680]{1,0:T(8,128)(2,1)} %velocities.3), custom_call_target="tpu_custom_call" | custom-call | flops 4026531840 | bytes 19660800 | tf_op jit(solution)/shard_map/project/pallas_call | solution.py:221
  25.5 4.9 %collective-permute-done.7 = f32[256,256]{1,0:T(8,128)S(1)} collective-permute-done((f32[256,256]{1,0:T(8,128)S(1)}, f32[256,256]{1,0:T(8,128)S(1)}, u32[]{:S(2)}, u32[]{:S(2)}) %collective-permute-start.7) | collective-permute-done | bytes 262176 | tf_op jit(solution)/shard_map/ppermute | solution.py:24
  30.4 0.4 collective-permute-start.8
  30.9 1.7 %collective-permute-start = (f32[256,256]{1,0:T(8,128)S(1)}, f32[256,256]{1,0:T(8,128)S(1)}, u32[]{:S(2)}, u32[]{:S(2)}) collective-permute-start(f32[256,256]{1,0:T(8,128)S(1)} %get-tuple-element.26), channel_id=1, source_target_pairs={{0,16},{8,24},{16,0},{24,8},{1,17},{9,25},{17,1},{25,9},{2,18},{10... | collective-permute-start | bytes 786440 | tf_op jit(solution)/shard_map/ppermute | solution.py:24
  32.5 0.0 collective-permute-done.1
  32.6 1.6 %collective-permute-start.2 = (f32[256,256]{1,0:T(8,128)S(1)}, f32[256,256]{1,0:T(8,128)S(1)}, u32[]{:S(2)}, u32[]{:S(2)}) collective-permute-start(f32[256,256]{1,0:T(8,128)S(1)} %add.55), channel_id=1, source_target_pairs={{0,8},{8,0},{16,24},{24,16},{1,9},{9,1},{17,25},{25,17},{2,10},{10... | collective-permute-start | bytes 786440 | tf_op jit(solution)/shard_map/ppermute | solution.py:24
  34.1 0.0 collective-permute-done.6
  34.1 5.5 %collective-permute-done.8 = f32[256,256]{1,0:T(8,128)S(1)} collective-permute-done((f32[256,256]{1,0:T(8,128)S(1)}, f32[256,256]{1,0:T(8,128)S(1)}, u32[]{:S(2)}, u32[]{:S(2)}) %collective-permute-start.8) | collective-permute-done | bytes 262176 | tf_op jit(solution)/shard_map/ppermute | solution.py:24
  39.7 0.1 fusion.2
  39.7 0.1 multiply_reduce_fusion.1
  39.8 3.2 %collective-permute-done = f32[256,256]{1,0:T(8,128)S(1)} collective-permute-done((f32[256,256]{1,0:T(8,128)S(1)}, f32[256,256]{1,0:T(8,128)S(1)}, u32[]{:S(2)}, u32[]{:S(2)}) %collective-permute-start) | collective-permute-done | bytes 262176 | tf_op jit(solution)/shard_map/ppermute | solution.py:24
  43.0 0.0 collective-permute-done.2
  43.0 0.1 multiply_reduce_fusion
  43.1 1.6 %collective-permute-start.9 = (f32[256]{0:T(256)S(1)}, f32[256]{0:T(256)S(1)}, u32[]{:S(2)}, u32[]{:S(2)}) collective-permute-start(f32[256]{0:T(256)S(1)} %add.60), channel_id=1, source_target_pairs={{0,2},{1,3},{2,0},{3,1},{4,6},{5,7},{6,4},{7,5},{8,10},{9,11},{10,... | collective-permute-start | bytes 3080 | tf_op jit(solution)/shard_map/ppermute | solution.py:24
  44.8 2.0 %collective-permute-done.9 = f32[256]{0:T(256)S(1)} collective-permute-done((f32[256]{0:T(256)S(1)}, f32[256]{0:T(256)S(1)}, u32[]{:S(2)}, u32[]{:S(2)}) %collective-permute-start.9) | collective-permute-done | bytes 1056 | tf_op jit(solution)/shard_map/ppermute | solution.py:24
  46.8 2.6 %collective-permute-start.10 = (f32[256]{0:T(256)S(1)}, f32[256]{0:T(256)S(1)}, u32[]{:S(2)}, u32[]{:S(2)}) collective-permute-start(f32[256]{0:T(256)S(1)} %add.61), channel_id=1, source_target_pairs={{0,4},{1,5},{2,6},{3,7},{4,0},{5,1},{6,2},{7,3},{8,12},{9,13},{10,... | collective-permute-start | bytes 3080 | tf_op jit(solution)/shard_map/ppermute | solution.py:24
  49.3 1.9 %collective-permute-done.10 = f32[256]{0:T(256)S(1)} collective-permute-done((f32[256]{0:T(256)S(1)}, f32[256]{0:T(256)S(1)}, u32[]{:S(2)}, u32[]{:S(2)}) %collective-permute-start.10) | collective-permute-done | bytes 1056 | tf_op jit(solution)/shard_map/ppermute | solution.py:24
  51.2 0.0 collective-permute-start.11
  51.2 3.6 %collective-permute-start.20 = (bf16[256,256]{1,0:T(8,128)(2,1)S(1)}, bf16[256,256]{1,0:T(8,128)(2,1)S(1)}, u32[]{:S(2)}, u32[]{:S(2)}) collective-permute-start(bf16[256,256]{1,0:T(8,128)(2,1)S(1)} %get-tuple-element.43), channel_id=1, source_target_pairs={{0,6},{1,7},{2,4},{3,5},{4,2},{5,3},{6,0},{7,1},{8,14},{9,15},{10,... | collective-permute-start | bytes 393224 | tf_op jit(solution)/shard_map/ppermute | solution.py:24
  54.8 0.0 collective-permute-start.19
  54.8 0.8 collective-permute-start.18
  55.6 0.0 collective-permute-done.11
  55.6 0.1 multiply_convert_fusion
  55.7 3.8 %collective-permute-done.20 = bf16[256,256]{1,0:T(8,128)(2,1)S(1)} collective-permute-done((bf16[256,256]{1,0:T(8,128)(2,1)S(1)}, bf16[256,256]{1,0:T(8,128)(2,1)S(1)}, u32[]{:S(2)}, u32[]{:S(2)}) %collective-permute-start.20) | collective-permute-done | bytes 131104 | tf_op jit(solution)/shard_map/ppermute | solution.py:24
  59.5 7.1 %collective-permute-done.19 = bf16[256,256]{1,0:T(8,128)(2,1)S(1)} collective-permute-done((bf16[256,256]{1,0:T(8,128)(2,1)S(1)}, bf16[256,256]{1,0:T(8,128)(2,1)S(1)}, u32[]{:S(2)}, u32[]{:S(2)}) %collective-permute-start.19) | collective-permute-done | bytes 131104 | tf_op jit(solution)/shard_map/ppermute | solution.py:24
  66.6 0.0 collective-permute-done.18
  66.6 0.1 pad_maximum_fusion.1
  66.7 1.5 %collective-permute-start.23 = (bf16[256,256]{1,0:T(8,128)(2,1)S(1)}, bf16[256,256]{1,0:T(8,128)(2,1)S(1)}, u32[]{:S(2)}, u32[]{:S(2)}) collective-permute-start(bf16[256,256]{1,0:T(8,128)(2,1)S(1)} %get-tuple-element.49), channel_id=1, source_target_pairs={{0,24},{8,16},{16,8},{24,0},{1,25},{9,17},{17,9},{25,1},{2,26},{10... | collective-permute-start | bytes 393224 | tf_op jit(solution)/shard_map/ppermute | solution.py:24
  68.2 1.5 %collective-permute-start.22 = (bf16[256,256]{1,0:T(8,128)(2,1)S(1)}, bf16[256,256]{1,0:T(8,128)(2,1)S(1)}, u32[]{:S(2)}, u32[]{:S(2)}) collective-permute-start(bf16[256,256]{1,0:T(8,128)(2,1)S(1)} %get-tuple-element.50), channel_id=1, source_target_pairs={{0,16},{8,24},{16,0},{24,8},{1,17},{9,25},{17,1},{25,9},{2,18},{10... | collective-permute-start | bytes 393224 | tf_op jit(solution)/shard_map/ppermute | solution.py:24
  69.7 0.5 collective-permute-start.21
  70.3 0.2 concatenate.3.refs_0_
  70.5 1.5 %collective-permute-start.14 = (bf16[528,256]{1,0:T(8,128)(2,1)S(1)}, bf16[528,256]{1,0:T(8,128)(2,1)S(1)}, u32[]{:S(2)}, u32[]{:S(2)}) collective-permute-start(bf16[528,256]{1,0:T(8,128)(2,1)S(1)} %concatenate.3.refs_0_), channel_id=1, source_target_pairs={{0,24},{8,16},{16,8},{24,0},{1,25},{9,17},{17,9},{25,1},{2,26},{10... | collective-permute-start | bytes 811016 | tf_op jit(solution)/shard_map/ppermute | solution.py:24
  72.0 1.5 %collective-permute-start.13 = (bf16[528,256]{1,0:T(8,128)(2,1)S(1)}, bf16[528,256]{1,0:T(8,128)(2,1)S(1)}, u32[]{:S(2)}, u32[]{:S(2)}) collective-permute-start(bf16[528,256]{1,0:T(8,128)(2,1)S(1)} %concatenate.3.refs_0_), channel_id=1, source_target_pairs={{0,16},{8,24},{16,0},{24,8},{1,17},{9,25},{17,1},{25,9},{2,18},{10... | collective-permute-start | bytes 811016 | tf_op jit(solution)/shard_map/ppermute | solution.py:24
  73.5 0.5 collective-permute-done.23.refs_3_
  74.0 7.5 %collective-permute-done.22.refs_2_ = bf16[256,256]{1,0:T(8,128)(2,1)S(1)} collective-permute-done((bf16[256,256]{1,0:T(8,128)(2,1)S(1)}, bf16[256,256]{1,0:T(8,128)(2,1)S(1)}, u32[]{:S(2)}, u32[]{:S(2)}) %collective-permute-start.22) | collective-permute-done | bytes 131104 | tf_op jit(solution)/shard_map/ppermute | solution.py:24
  81.5 0.0 collective-permute-done.21.refs_1_
  81.5 0.1 pad_maximum_fusion.2
  81.6 0.1 collective-permute-start.24
  81.7 1.5 %collective-permute-start.12 = (bf16[528,256]{1,0:T(8,128)(2,1)S(1)}, bf16[528,256]{1,0:T(8,128)(2,1)S(1)}, u32[]{:S(2)}, u32[]{:S(2)}) collective-permute-start(bf16[528,256]{1,0:T(8,128)(2,1)S(1)} %concatenate.3.refs_0_), channel_id=1, source_target_pairs={{0,8},{8,0},{16,24},{24,16},{1,9},{9,1},{17,25},{25,17},{2,10},{10... | collective-permute-start | bytes 811016 | tf_op jit(solution)/shard_map/ppermute | solution.py:24
  83.2 2.5 %collective-permute-start.5 = (bf16[256,256]{1,0:T(8,128)(2,1)S(1)}, bf16[256,256]{1,0:T(8,128)(2,1)S(1)}, u32[]{:S(2)}, u32[]{:S(2)}) collective-permute-start(bf16[256,256]{1,0:T(8,128)(2,1)S(1)} %get-tuple-element.33), channel_id=1, source_target_pairs={{0,6},{1,7},{2,4},{3,5},{4,2},{5,3},{6,0},{7,1},{8,14},{9,15},{10,... | collective-permute-start | bytes 393224 | tf_op jit(solution)/shard_map/ppermute | solution.py:24
  85.6 0.0 collective-permute-done.14.refs_3_
  85.6 0.0 collective-permute-start.4
  85.6 1.5 %collective-permute-done.13.refs_2_ = bf16[528,256]{1,0:T(8,128)(2,1)S(1)} collective-permute-done((bf16[528,256]{1,0:T(8,128)(2,1)S(1)}, bf16[528,256]{1,0:T(8,128)(2,1)S(1)}, u32[]{:S(2)}, u32[]{:S(2)}) %collective-permute-start.13) | collective-permute-done | bytes 270368 | tf_op jit(solution)/shard_map/ppermute | solution.py:24
  87.1 0.4 collective-permute-start.3
  87.6 3.0 %collective-permute-done.12.refs_1_ = bf16[528,256]{1,0:T(8,128)(2,1)S(1)} collective-permute-done((bf16[528,256]{1,0:T(8,128)(2,1)S(1)}, bf16[528,256]{1,0:T(8,128)(2,1)S(1)}, u32[]{:S(2)}, u32[]{:S(2)}) %collective-permute-start.12) | collective-permute-done | bytes 270368 | tf_op jit(solution)/shard_map/ppermute | solution.py:24
  90.6 2.8 %shift.1.refs_5_ = bf16[8,1024,512]{2,1,0:T(8,128)(2,1)S(1)} custom-call(s32[8]{0:T(128)S(1)} %copy-done, bf16[528,256]{1,0:T(8,128)(2,1)S(1)} %concatenate.3.refs_0_, bf16[528,256]{1,0:T(8,128)(2,1)S(1)} %collective-permute-done.12.refs_1_, bf16[528,256]{1,0:T(8,128)(2,1)S(1)} %collective-permute-done.13.refs_2_, ...), custom_call_target="tpu_custom_call" | custom-call | bytes 9437184 | tf_op jit(solution)/shard_map/shift/pallas_call | solution.py:284
  93.4 0.0 collective-permute-done.5
  93.4 3.0 %collective-permute-done.4 = bf16[256,256]{1,0:T(8,128)(2,1)S(1)} collective-permute-done((bf16[256,256]{1,0:T(8,128)(2,1)S(1)}, bf16[256,256]{1,0:T(8,128)(2,1)S(1)}, u32[]{:S(2)}, u32[]{:S(2)}) %collective-permute-start.4) | collective-permute-done | bytes 131104 | tf_op jit(solution)/shard_map/ppermute | solution.py:24
  96.4 0.1 pad_maximum_fusion
  96.6 0.8 collective-permute-start.17
  97.4 1.3 %collective-permute-start.16 = (bf16[256,256]{1,0:T(8,128)(2,1)S(1)}, bf16[256,256]{1,0:T(8,128)(2,1)S(1)}, u32[]{:S(2)}, u32[]{:S(2)}) collective-permute-start(bf16[256,256]{1,0:T(8,128)(2,1)S(1)} %get-tuple-element.54), channel_id=1, source_target_pairs={{0,16},{8,24},{16,0},{24,8},{1,17},{9,25},{17,1},{25,9},{2,18},{10... | collective-permute-start | bytes 393224 | tf_op jit(solution)/shard_map/ppermute | solution.py:24
  98.7 1.4 %collective-permute-start.15 = (bf16[256,256]{1,0:T(8,128)(2,1)S(1)}, bf16[256,256]{1,0:T(8,128)(2,1)S(1)}, u32[]{:S(2)}, u32[]{:S(2)}) collective-permute-start(bf16[256,256]{1,0:T(8,128)(2,1)S(1)} %get-tuple-element.55), channel_id=1, source_target_pairs={{0,8},{8,0},{16,24},{24,16},{1,9},{9,1},{17,25},{25,17},{2,10},{10... | collective-permute-start | bytes 393224 | tf_op jit(solution)/shard_map/ppermute | solution.py:24
  100.1 0.0 collective-permute-done.24.refs_4_
  100.1 7.6 %correlate.2.refs_6_ = f32[8,1024,512]{2,1,0:T(8,128)} custom-call(f32[8]{0:T(128)S(1)} %convert_rsqrt_fusion.factors, bf16[256,256]{1,0:T(8,128)(2,1)S(1)} %bitcast.30, bf16[256,256]{1,0:T(8,128)(2,1)S(1)} %collective-permute-done.21.refs_1_, bf16[256,256]{1,0:T(8,128)(2,1)S(1)} %collective-permute-done.22.refs_2_, ...), custom_call_target="tpu_custom_call" | custom-call | flops 4294967296 | bytes 16777216 | tf_op jit(solution)/shard_map/correlate/pallas_call | solution.py:364
  107.8 0.0 collective-permute-done.16.refs_2_
  107.8 0.0 collective-permute-done.15.refs_1_
  107.8 0.1 pad_maximum_fusion.3
  107.9 0.1 collective-permute-start.25
  107.9 1.9 %collective-permute-done.25.refs_4_ = bf16[4,256,256]{2,1,0:T(8,128)(2,1)S(1)} collective-permute-done((bf16[4,256,256]{2,1,0:T(8,128)(2,1)S(1)}, bf16[4,256,256]{2,1,0:T(8,128)(2,1)S(1)}, u32[]{:S(2)}, u32[]{:S(2)}) %collective-permute-start.25) | collective-permute-done | bytes 524320 | tf_op jit(solution)/shard_map/ppermute | solution.py:24
  109.8 7.6 %correlate.3 = f32[8,1024,512]{2,1,0:T(8,128)} custom-call(f32[8]{0:T(128)S(1)} %convert_rsqrt_fusion.factors, bf16[256,256]{1,0:T(8,128)(2,1)S(1)} %get-tuple-element.37.refs_0_, bf16[256,256]{1,0:T(8,128)(2,1)S(1)} %collective-permute-done.15.refs_1_, bf16[256,256]{1,0:T(8,128)(2,1)S(1)} %collective-permute-done.16.refs_2_, ...), custom_call_target="tpu_custom_call", output_to_operand_aliasing={{}: (7, {})} | custom-call | flops 4294967296 | bytes 16777216 | tf_op jit(solution)/shard_map/correlate/pallas_call | solution.py:364
  (18 shorter events, 0.2 us)
Async XLA Ops:
  14.0 18.5 %collective-permute-start.1 = (f32[256,256]{1,0:T(8,128)S(1)}, f32[256,256]{1,0:T(8,128)S(1)}, u32[]{:S(2)}, u32[]{:S(2)}) collective-permute-start(f32[256,256]{1,0:T(8,128)S(1)} %get-tuple-element.28), channel_id=1, source_target_pairs={{0,16},{8,24},{16,0},{24,8},{1,17},{9,25},{17,1},{25,9},{2,18},{10... | collective-permute-start | bytes 786440 | tf_op jit(solution)/shard_map/ppermute | solution.py:24
  17.0 17.1 %collective-permute-start.6 = (f32[256,256]{1,0:T(8,128)S(1)}, f32[256,256]{1,0:T(8,128)S(1)}, u32[]{:S(2)}, u32[]{:S(2)}) collective-permute-start(f32[256,256]{1,0:T(8,128)S(1)} %get-tuple-element.30), channel_id=1, source_target_pairs={{0,8},{8,0},{16,24},{24,16},{1,9},{9,1},{17,25},{25,17},{2,10},{10... | collective-permute-start | bytes 786440 | tf_op jit(solution)/shard_map/ppermute | solution.py:24
  18.5 11.9 %collective-permute-start.7 = (f32[256,256]{1,0:T(8,128)S(1)}, f32[256,256]{1,0:T(8,128)S(1)}, u32[]{:S(2)}, u32[]{:S(2)}) collective-permute-start(f32[256,256]{1,0:T(8,128)S(1)} %get-tuple-element.32), channel_id=1, source_target_pairs={{0,8},{8,0},{16,24},{24,16},{1,9},{9,1},{17,25},{25,17},{2,10},{10... | collective-permute-start | bytes 786440 | tf_op jit(solution)/shard_map/ppermute | solution.py:24
  19.0 68.5 %copy-start = (s32[8]{0:T(128)S(1)}, s32[8]{0:T(128)}, u32[]{:S(2)}) copy-start(s32[8]{0:T(128)} %offsets.1) | copy-start | bytes 100
  30.4 9.2 %collective-permute-start.8 = (f32[256,256]{1,0:T(8,128)S(1)}, f32[256,256]{1,0:T(8,128)S(1)}, u32[]{:S(2)}, u32[]{:S(2)}) collective-permute-start(f32[256,256]{1,0:T(8,128)S(1)} %add.58), channel_id=1, source_target_pairs={{0,16},{8,24},{16,0},{24,8},{1,17},{9,25},{17,1},{25,9},{2,18},{10... | collective-permute-start | bytes 786440 | tf_op jit(solution)/shard_map/ppermute | solution.py:24
  30.9 12.2 %collective-permute-start = (f32[256,256]{1,0:T(8,128)S(1)}, f32[256,256]{1,0:T(8,128)S(1)}, u32[]{:S(2)}, u32[]{:S(2)}) collective-permute-start(f32[256,256]{1,0:T(8,128)S(1)} %get-tuple-element.26), channel_id=1, source_target_pairs={{0,16},{8,24},{16,0},{24,8},{1,17},{9,25},{17,1},{25,9},{2,18},{10... | collective-permute-start | bytes 786440 | tf_op jit(solution)/shard_map/ppermute | solution.py:24
  32.6 10.5 %collective-permute-start.2 = (f32[256,256]{1,0:T(8,128)S(1)}, f32[256,256]{1,0:T(8,128)S(1)}, u32[]{:S(2)}, u32[]{:S(2)}) collective-permute-start(f32[256,256]{1,0:T(8,128)S(1)} %add.55), channel_id=1, source_target_pairs={{0,8},{8,0},{16,24},{24,16},{1,9},{9,1},{17,25},{25,17},{2,10},{10... | collective-permute-start | bytes 786440 | tf_op jit(solution)/shard_map/ppermute | solution.py:24
  43.1 3.6 %collective-permute-start.9 = (f32[256]{0:T(256)S(1)}, f32[256]{0:T(256)S(1)}, u32[]{:S(2)}, u32[]{:S(2)}) collective-permute-start(f32[256]{0:T(256)S(1)} %add.60), channel_id=1, source_target_pairs={{0,2},{1,3},{2,0},{3,1},{4,6},{5,7},{6,4},{7,5},{8,10},{9,11},{10,... | collective-permute-start | bytes 3080 | tf_op jit(solution)/shard_map/ppermute | solution.py:24
  46.8 4.5 %collective-permute-start.10 = (f32[256]{0:T(256)S(1)}, f32[256]{0:T(256)S(1)}, u32[]{:S(2)}, u32[]{:S(2)}) collective-permute-start(f32[256]{0:T(256)S(1)} %add.61), channel_id=1, source_target_pairs={{0,4},{1,5},{2,6},{3,7},{4,0},{5,1},{6,2},{7,3},{8,12},{9,13},{10,... | collective-permute-start | bytes 3080 | tf_op jit(solution)/shard_map/ppermute | solution.py:24
  51.2 4.4 %collective-permute-start.11 = (f32[256]{0:T(256)S(1)}, f32[256]{0:T(256)S(1)}, u32[]{:S(2)}, u32[]{:S(2)}) collective-permute-start(f32[256]{0:T(256)S(1)} %add.62), channel_id=1, source_target_pairs={{0,1},{1,0},{2,3},{3,2},{4,5},{5,4},{6,7},{7,6},{8,9},{9,8},{10,11... | collective-permute-start | bytes 3080 | tf_op jit(solution)/shard_map/ppermute | solution.py:24
  51.2 8.3 %collective-permute-start.20 = (bf16[256,256]{1,0:T(8,128)(2,1)S(1)}, bf16[256,256]{1,0:T(8,128)(2,1)S(1)}, u32[]{:S(2)}, u32[]{:S(2)}) collective-permute-start(bf16[256,256]{1,0:T(8,128)(2,1)S(1)} %get-tuple-element.43), channel_id=1, source_target_pairs={{0,6},{1,7},{2,4},{3,5},{4,2},{5,3},{6,0},{7,1},{8,14},{9,15},{10,... | collective-permute-start | bytes 393224 | tf_op jit(solution)/shard_map/ppermute | solution.py:24
  54.8 11.7 %collective-permute-start.19 = (bf16[256,256]{1,0:T(8,128)(2,1)S(1)}, bf16[256,256]{1,0:T(8,128)(2,1)S(1)}, u32[]{:S(2)}, u32[]{:S(2)}) collective-permute-start(bf16[256,256]{1,0:T(8,128)(2,1)S(1)} %get-tuple-element.43), channel_id=1, source_target_pairs={{0,4},{1,5},{2,6},{3,7},{4,0},{5,1},{6,2},{7,3},{8,12},{9,13},{10,... | collective-permute-start | bytes 393224 | tf_op jit(solution)/shard_map/ppermute | solution.py:24
  54.8 11.7 %collective-permute-start.18 = (bf16[256,256]{1,0:T(8,128)(2,1)S(1)}, bf16[256,256]{1,0:T(8,128)(2,1)S(1)}, u32[]{:S(2)}, u32[]{:S(2)}) collective-permute-start(bf16[256,256]{1,0:T(8,128)(2,1)S(1)} %get-tuple-element.43), channel_id=1, source_target_pairs={{0,2},{1,3},{2,0},{3,1},{4,6},{5,7},{6,4},{7,5},{8,10},{9,11},{10,... | collective-permute-start | bytes 393224 | tf_op jit(solution)/shard_map/ppermute | solution.py:24
  66.7 7.3 %collective-permute-start.23 = (bf16[256,256]{1,0:T(8,128)(2,1)S(1)}, bf16[256,256]{1,0:T(8,128)(2,1)S(1)}, u32[]{:S(2)}, u32[]{:S(2)}) collective-permute-start(bf16[256,256]{1,0:T(8,128)(2,1)S(1)} %get-tuple-element.49), channel_id=1, source_target_pairs={{0,24},{8,16},{16,8},{24,0},{1,25},{9,17},{17,9},{25,1},{2,26},{10... | collective-permute-start | bytes 393224 | tf_op jit(solution)/shard_map/ppermute | solution.py:24
  68.2 13.3 %collective-permute-start.22 = (bf16[256,256]{1,0:T(8,128)(2,1)S(1)}, bf16[256,256]{1,0:T(8,128)(2,1)S(1)}, u32[]{:S(2)}, u32[]{:S(2)}) collective-permute-start(bf16[256,256]{1,0:T(8,128)(2,1)S(1)} %get-tuple-element.50), channel_id=1, source_target_pairs={{0,16},{8,24},{16,0},{24,8},{1,17},{9,25},{17,1},{25,9},{2,18},{10... | collective-permute-start | bytes 393224 | tf_op jit(solution)/shard_map/ppermute | solution.py:24
  69.7 11.8 %collective-permute-start.21 = (bf16[256,256]{1,0:T(8,128)(2,1)S(1)}, bf16[256,256]{1,0:T(8,128)(2,1)S(1)}, u32[]{:S(2)}, u32[]{:S(2)}) collective-permute-start(bf16[256,256]{1,0:T(8,128)(2,1)S(1)} %get-tuple-element.51), channel_id=1, source_target_pairs={{0,8},{8,0},{16,24},{24,16},{1,9},{9,1},{17,25},{25,17},{2,10},{10... | collective-permute-start | bytes 393224 | tf_op jit(solution)/shard_map/ppermute | solution.py:24
  70.5 15.2 %collective-permute-start.14 = (bf16[528,256]{1,0:T(8,128)(2,1)S(1)}, bf16[528,256]{1,0:T(8,128)(2,1)S(1)}, u32[]{:S(2)}, u32[]{:S(2)}) collective-permute-start(bf16[528,256]{1,0:T(8,128)(2,1)S(1)} %concatenate.3.refs_0_), channel_id=1, source_target_pairs={{0,24},{8,16},{16,8},{24,0},{1,25},{9,17},{17,9},{25,1},{2,26},{10... | collective-permute-start | bytes 811016 | tf_op jit(solution)/shard_map/ppermute | solution.py:24
  72.0 15.1 %collective-permute-start.13 = (bf16[528,256]{1,0:T(8,128)(2,1)S(1)}, bf16[528,256]{1,0:T(8,128)(2,1)S(1)}, u32[]{:S(2)}, u32[]{:S(2)}) collective-permute-start(bf16[528,256]{1,0:T(8,128)(2,1)S(1)} %concatenate.3.refs_0_), channel_id=1, source_target_pairs={{0,16},{8,24},{16,0},{24,8},{1,17},{9,25},{17,1},{25,9},{2,18},{10... | collective-permute-start | bytes 811016 | tf_op jit(solution)/shard_map/ppermute | solution.py:24
  81.6 18.5 %collective-permute-start.24 = (bf16[4,256,256]{2,1,0:T(8,128)(2,1)S(1)}, bf16[4,256,256]{2,1,0:T(8,128)(2,1)S(1)}, u32[]{:S(2)}, u32[]{:S(2)}) collective-permute-start(bf16[4,256,256]{2,1,0:T(8,128)(2,1)S(1)} %pad_maximum_fusion.2), channel_id=1, source_target_pairs={{0,1},{1,0},{2,3},{3,2},{4,5},{5,4},{6,7},{7,6},{8,9},{9,8},{10,11... | collective-permute-start | bytes 1572872 | tf_op jit(solution)/shard_map/ppermute | solution.py:24
  81.7 8.9 %collective-permute-start.12 = (bf16[528,256]{1,0:T(8,128)(2,1)S(1)}, bf16[528,256]{1,0:T(8,128)(2,1)S(1)}, u32[]{:S(2)}, u32[]{:S(2)}) collective-permute-start(bf16[528,256]{1,0:T(8,128)(2,1)S(1)} %concatenate.3.refs_0_), channel_id=1, source_target_pairs={{0,8},{8,0},{16,24},{24,16},{1,9},{9,1},{17,25},{25,17},{2,10},{10... | collective-permute-start | bytes 811016 | tf_op jit(solution)/shard_map/ppermute | solution.py:24
  83.2 10.3 %collective-permute-start.5 = (bf16[256,256]{1,0:T(8,128)(2,1)S(1)}, bf16[256,256]{1,0:T(8,128)(2,1)S(1)}, u32[]{:S(2)}, u32[]{:S(2)}) collective-permute-start(bf16[256,256]{1,0:T(8,128)(2,1)S(1)} %get-tuple-element.33), channel_id=1, source_target_pairs={{0,6},{1,7},{2,4},{3,5},{4,2},{5,3},{6,0},{7,1},{8,14},{9,15},{10,... | collective-permute-start | bytes 393224 | tf_op jit(solution)/shard_map/ppermute | solution.py:24
  85.6 10.8 %collective-permute-start.4 = (bf16[256,256]{1,0:T(8,128)(2,1)S(1)}, bf16[256,256]{1,0:T(8,128)(2,1)S(1)}, u32[]{:S(2)}, u32[]{:S(2)}) collective-permute-start(bf16[256,256]{1,0:T(8,128)(2,1)S(1)} %get-tuple-element.33), channel_id=1, source_target_pairs={{0,4},{1,5},{2,6},{3,7},{4,0},{5,1},{6,2},{7,3},{8,12},{9,13},{10,... | collective-permute-start | bytes 393224 | tf_op jit(solution)/shard_map/ppermute | solution.py:24
  87.1 9.3 %collective-permute-start.3 = (bf16[256,256]{1,0:T(8,128)(2,1)S(1)}, bf16[256,256]{1,0:T(8,128)(2,1)S(1)}, u32[]{:S(2)}, u32[]{:S(2)}) collective-permute-start(bf16[256,256]{1,0:T(8,128)(2,1)S(1)} %get-tuple-element.33), channel_id=1, source_target_pairs={{0,2},{1,3},{2,0},{3,1},{4,6},{5,7},{6,4},{7,5},{8,10},{9,11},{10,... | collective-permute-start | bytes 393224 | tf_op jit(solution)/shard_map/ppermute | solution.py:24
  96.6 11.2 %collective-permute-start.17 = (bf16[256,256]{1,0:T(8,128)(2,1)S(1)}, bf16[256,256]{1,0:T(8,128)(2,1)S(1)}, u32[]{:S(2)}, u32[]{:S(2)}) collective-permute-start(bf16[256,256]{1,0:T(8,128)(2,1)S(1)} %get-tuple-element.53), channel_id=1, source_target_pairs={{0,24},{8,16},{16,8},{24,0},{1,25},{9,17},{17,9},{25,1},{2,26},{10... | collective-permute-start | bytes 393224 | tf_op jit(solution)/shard_map/ppermute | solution.py:24
  97.4 10.4 %collective-permute-start.16 = (bf16[256,256]{1,0:T(8,128)(2,1)S(1)}, bf16[256,256]{1,0:T(8,128)(2,1)S(1)}, u32[]{:S(2)}, u32[]{:S(2)}) collective-permute-start(bf16[256,256]{1,0:T(8,128)(2,1)S(1)} %get-tuple-element.54), channel_id=1, source_target_pairs={{0,16},{8,24},{16,0},{24,8},{1,17},{9,25},{17,1},{25,9},{2,18},{10... | collective-permute-start | bytes 393224 | tf_op jit(solution)/shard_map/ppermute | solution.py:24
  98.7 9.1 %collective-permute-start.15 = (bf16[256,256]{1,0:T(8,128)(2,1)S(1)}, bf16[256,256]{1,0:T(8,128)(2,1)S(1)}, u32[]{:S(2)}, u32[]{:S(2)}) collective-permute-start(bf16[256,256]{1,0:T(8,128)(2,1)S(1)} %get-tuple-element.55), channel_id=1, source_target_pairs={{0,8},{8,0},{16,24},{24,16},{1,9},{9,1},{17,25},{25,17},{2,10},{10... | collective-permute-start | bytes 393224 | tf_op jit(solution)/shard_map/ppermute | solution.py:24
  107.9 2.0 %collective-permute-start.25 = (bf16[4,256,256]{2,1,0:T(8,128)(2,1)S(1)}, bf16[4,256,256]{2,1,0:T(8,128)(2,1)S(1)}, u32[]{:S(2)}, u32[]{:S(2)}) collective-permute-start(bf16[4,256,256]{2,1,0:T(8,128)(2,1)S(1)} %pad_maximum_fusion.3), channel_id=1, source_target_pairs={{0,1},{1,0},{2,3},{3,2},{4,5},{5,4},{6,7},{7,6},{8,9},{9,8},{10,11... | collective-permute-start | bytes 1572872 | tf_op jit(solution)/shard_map/ppermute | solution.py:24

commit v2 on v1

--- a/solution.py
+++ b/solution.py
@@ -48,7 +48,7 @@
             ] = jnp.concatenate(tiles, axis=0).astype(jnp.bfloat16)
         return carry
 
-    lax.fori_loop(0, groups, move, 0, unroll=2)
+    lax.fori_loop(0, groups, move, 0)
 
 
 def arrangement(lists):
@@ -412,11 +412,14 @@
 
     bits = [1 << b for b in range(ranks.bit_length() - 1)]
     orders = [bits, bits[::-1]]
-    early = [[m for m in range(ranks) if m & order[0]] for order in orders]
-    late = [[m for m in range(ranks) if not m & order[0]] for order in orders]
-    early_parts, ordered = reorder_project(modes_panel, velocities, atom_slot, early, size)
-    late_parts = project(ordered, velocities, late, size)
-    halves = [reduce_scatter(early_parts[h] | late_parts[h], orders[h]) for h in range(2)]
+    onward = [[m for m in range(ranks) if m & order[0] and m ^ order[0]] for order in orders]
+    final = [[order[0]] for order in orders]
+    meeting = [[m for m in range(1, ranks) if not m & order[0]] for order in orders]
+    parts, ordered = reorder_project(modes_panel, velocities, atom_slot, onward, size)
+    for lists in (final, meeting, [[0], [0]]):
+        more = project(ordered, velocities, lists, size)
+        parts = [parts[h] | more[h] for h in range(2)]
+    halves = [reduce_scatter(parts[h], orders[h]) for h in range(2)]
 
     raw = [half.astype(jnp.bfloat16) for half in halves]
     across = []

time: 118 us -> 112 us (0.949)
  waiting for transfers between devices: 45.9 us -> 37.7 us
  Pallas kernels: 38.5 us -> 41.6 us
    ppermute x26, waiting for transfers between devices: 45.9 us -> 37.7 us  [swap(): return lax.ppermute(block, axis, [(i, i ^ offset) for i in range(size)])]
    pallas_call x1 -> x3, Pallas kernels: 6.43 us -> 12.1 us  [project(): pl.pallas_call(functools.partial(project_kernel, chunk=chunk, order=order...]
    pallas_call x1, Pallas kernels: 14 us -> 11.5 us  [reorder_project(): pl.pallas_call(functools.partial(reorder_project_kernel, chunk=chunk, blo...]
  transfers between devices with their start and end apart: 26 -> 26, of which waited for: 13 -> 12; matrix products, arithmetic and copies ran while one was open for 1% -> 1% of each run, Pallas kernels for 14% -> 20%
where the time goes in v2:
time: 112 us
  Pallas kernels  41.6 us (37%)
  waiting for transfers between devices  37.7 us (34%)
  starting transfers between devices  31.7 us (28%)
    ppermute x26, waiting for transfers between devices, swap(): return lax.ppermute(block, axis, [(i, i ^ offset) for i in range(size)])  37.7 us
    ppermute x26, starting transfers between devices, swap(): return lax.ppermute(block, axis, [(i, i ^ offset) for i in range(size)])  31.7 us
    pallas_call x2, Pallas kernels, correlate(): pl.pallas_call(functools.partial(correlate_kernel, parts=parts, owners=ow...  15.2 us
    pallas_call x3, Pallas kernels, project(): pl.pallas_call(functools.partial(project_kernel, chunk=chunk, order=order...  12.1 us
    pallas_call x1, Pallas kernels, reorder_project(): pl.pallas_call(functools.partial(reorder_project_kernel, chunk=chunk, blo...  11.5 us
    pallas_call x1, Pallas kernels, shifted_copies(): pl.pallas_call(functools.partial(shift_kernel, parts=parts), out_shape=ja...  2.85 us
  transfers between devices with their start and end apart: 26, of which 12 were waited for; matrix products, arithmetic and copies ran while one was open for 1% of the time, Pallas kernels for 20%

profile of v2, /device:TPU:0, one launch (start us, length us, event | category | flops | bytes accessed | tf_op | source)
XLA Modules:
  0.0 112.2 jit_solution(3745794553796654728)
XLA Ops:
  0.0 11.5 %reorder_project.1 = (f32[256,256]{1,0:T(8,128)S(1)}, f32[256,256]{1,0:T(8,128)S(1)}, bf16[7680,512]{1,0:T(8,128)(2,1)S(1)}) custom-call(s32[2560]{0:T(1024)} %slot.1, bf16[7680,512]{1,0:T(8,128)(2,1)} %panel.1, bf16[1024,7680]{1,0:T(8,128)(2,1)} %velocities.7), custom_call_target="tpu_custom_call" | custom-call | flops 2013265920 | bytes 19660800 | tf_op jit(solution)/shard_map/reorder_project/pallas_call | solution.py:153
  11.5 3.1 %collective-permute-start.1 = (f32[256,256]{1,0:T(8,128)S(1)}, f32[256,256]{1,0:T(8,128)S(1)}, u32[]{:S(2)}, u32[]{:S(2)}) collective-permute-start(f32[256,256]{1,0:T(8,128)S(1)} %get-tuple-element.28), channel_id=1, source_target_pairs={{0,16},{8,24},{16,0},{24,8},{1,17},{9,25},{17,1},{25,9},{2,18},{10... | collective-permute-start | bytes 786440 | tf_op jit(solution)/shard_map/ppermute | solution.py:24
  14.6 1.4 %collective-permute-start.7 = (f32[256,256]{1,0:T(8,128)S(1)}, f32[256,256]{1,0:T(8,128)S(1)}, u32[]{:S(2)}, u32[]{:S(2)}) collective-permute-start(f32[256,256]{1,0:T(8,128)S(1)} %get-tuple-element.32), channel_id=1, source_target_pairs={{0,8},{8,0},{16,24},{24,16},{1,9},{9,1},{17,25},{25,17},{2,10},{10... | collective-permute-start | bytes 786440 | tf_op jit(solution)/shard_map/ppermute | solution.py:24
  16.0 4.1 %project.4 = (f32[256,256]{1,0:T(8,128)S(1)}, f32[256,256]{1,0:T(8,128)S(1)}) custom-call(bf16[7680,512]{1,0:T(8,128)(2,1)S(1)} %get-tuple-element.24.panel, bf16[1024,7680]{1,0:T(8,128)(2,1)} %velocities.7), custom_call_target="tpu_custom_call" | custom-call | flops 2013265920 | bytes 15728640 | tf_op jit(solution)/shard_map/project/pallas_call | solution.py:221
  20.1 0.7 collective-permute-start.6
  20.8 4.1 %project.5 = (f32[256,256]{1,0:T(8,128)S(1)}, f32[256,256]{1,0:T(8,128)S(1)}) custom-call(bf16[7680,512]{1,0:T(8,128)(2,1)S(1)} %get-tuple-element.24.panel, bf16[1024,7680]{1,0:T(8,128)(2,1)} %velocities.7), custom_call_target="tpu_custom_call" | custom-call | flops 2013265920 | bytes 15728640 | tf_op jit(solution)/shard_map/project/pallas_call | solution.py:221
  24.9 0.0 collective-permute-done.7
  25.0 0.1 collective-permute-start.8
  25.1 1.9 %collective-permute-start = (f32[256,256]{1,0:T(8,128)S(1)}, f32[256,256]{1,0:T(8,128)S(1)}, u32[]{:S(2)}, u32[]{:S(2)}) collective-permute-start(f32[256,256]{1,0:T(8,128)S(1)} %get-tuple-element.26), channel_id=1, source_target_pairs={{0,16},{8,24},{16,0},{24,8},{1,17},{9,25},{17,1},{25,9},{2,18},{10... | collective-permute-start | bytes 786440 | tf_op jit(solution)/shard_map/ppermute | solution.py:24
  27.1 3.9 %project.3 = (f32[256,256]{1,0:T(8,128)S(1)}, f32[256,256]{1,0:T(8,128)S(1)}) custom-call(bf16[7680,512]{1,0:T(8,128)(2,1)S(1)} %get-tuple-element.24.panel, bf16[1024,7680]{1,0:T(8,128)(2,1)} %velocities.7), custom_call_target="tpu_custom_call" | custom-call | flops 2013265920 | bytes 11796480 | tf_op jit(solution)/shard_map/project/pallas_call | solution.py:221
  30.9 0.0 collective-permute-done.1
  31.0 1.5 %collective-permute-start.2 = (f32[256,256]{1,0:T(8,128)S(1)}, f32[256,256]{1,0:T(8,128)S(1)}, u32[]{:S(2)}, u32[]{:S(2)}) collective-permute-start(f32[256,256]{1,0:T(8,128)S(1)} %add.55), channel_id=1, source_target_pairs={{0,8},{8,0},{16,24},{24,16},{1,9},{9,1},{17,25},{25,17},{2,10},{10... | collective-permute-start | bytes 786440 | tf_op jit(solution)/shard_map/ppermute | solution.py:24
  32.4 0.0 collective-permute-done.6
  32.5 1.7 %collective-permute-done.8 = f32[256,256]{1,0:T(8,128)S(1)} collective-permute-done((f32[256,256]{1,0:T(8,128)S(1)}, f32[256,256]{1,0:T(8,128)S(1)}, u32[]{:S(2)}, u32[]{:S(2)}) %collective-permute-start.8) | collective-permute-done | bytes 262176 | tf_op jit(solution)/shard_map/ppermute | solution.py:24
  34.2 0.1 fusion.2
  34.3 0.1 multiply_reduce_fusion.1
  34.3 3.5 %collective-permute-done = f32[256,256]{1,0:T(8,128)S(1)} collective-permute-done((f32[256,256]{1,0:T(8,128)S(1)}, f32[256,256]{1,0:T(8,128)S(1)}, u32[]{:S(2)}, u32[]{:S(2)}) %collective-permute-start) | collective-permute-done | bytes 262176 | tf_op jit(solution)/shard_map/ppermute | solution.py:24
  37.9 0.0 collective-permute-done.2
  37.9 0.1 multiply_reduce_fusion
  37.9 1.6 %collective-permute-start.9 = (f32[256]{0:T(256)S(1)}, f32[256]{0:T(256)S(1)}, u32[]{:S(2)}, u32[]{:S(2)}) collective-permute-start(f32[256]{0:T(256)S(1)} %add.60), channel_id=1, source_target_pairs={{0,2},{1,3},{2,0},{3,1},{4,6},{5,7},{6,4},{7,5},{8,10},{9,11},{10,... | collective-permute-start | bytes 3080 | tf_op jit(solution)/shard_map/ppermute | solution.py:24
  39.6 2.0 %collective-permute-done.9 = f32[256]{0:T(256)S(1)} collective-permute-done((f32[256]{0:T(256)S(1)}, f32[256]{0:T(256)S(1)}, u32[]{:S(2)}, u32[]{:S(2)}) %collective-permute-start.9) | collective-permute-done | bytes 1056 | tf_op jit(solution)/shard_map/ppermute | solution.py:24
  41.6 2.6 %collective-permute-start.10 = (f32[256]{0:T(256)S(1)}, f32[256]{0:T(256)S(1)}, u32[]{:S(2)}, u32[]{:S(2)}) collective-permute-start(f32[256]{0:T(256)S(1)} %add.61), channel_id=1, source_target_pairs={{0,4},{1,5},{2,6},{3,7},{4,0},{5,1},{6,2},{7,3},{8,12},{9,13},{10,... | collective-permute-start | bytes 3080 | tf_op jit(solution)/shard_map/ppermute | solution.py:24
  44.2 1.9 %collective-permute-done.10 = f32[256]{0:T(256)S(1)} collective-permute-done((f32[256]{0:T(256)S(1)}, f32[256]{0:T(256)S(1)}, u32[]{:S(2)}, u32[]{:S(2)}) %collective-permute-start.10) | collective-permute-done | bytes 1056 | tf_op jit(solution)/shard_map/ppermute | solution.py:24
  46.1 0.0 collective-permute-start.11
  46.1 3.6 %collective-permute-start.20 = (bf16[256,256]{1,0:T(8,128)(2,1)S(1)}, bf16[256,256]{1,0:T(8,128)(2,1)S(1)}, u32[]{:S(2)}, u32[]{:S(2)}) collective-permute-start(bf16[256,256]{1,0:T(8,128)(2,1)S(1)} %get-tuple-element.43), channel_id=1, source_target_pairs={{0,6},{1,7},{2,4},{3,5},{4,2},{5,3},{6,0},{7,1},{8,14},{9,15},{10,... | collective-permute-start | bytes 393224 | tf_op jit(solution)/shard_map/ppermute | solution.py:24
  49.7 0.0 collective-permute-start.19
  49.7 0.8 collective-permute-start.18
  50.4 0.0 collective-permute-done.11
  50.5 0.1 multiply_convert_fusion
  50.5 3.8 %collective-permute-done.20 = bf16[256,256]{1,0:T(8,128)(2,1)S(1)} collective-permute-done((bf16[256,256]{1,0:T(8,128)(2,1)S(1)}, bf16[256,256]{1,0:T(8,128)(2,1)S(1)}, u32[]{:S(2)}, u32[]{:S(2)}) %collective-permute-start.20) | collective-permute-done | bytes 131104 | tf_op jit(solution)/shard_map/ppermute | solution.py:24
  54.3 7.1 %collective-permute-done.19 = bf16[256,256]{1,0:T(8,128)(2,1)S(1)} collective-permute-done((bf16[256,256]{1,0:T(8,128)(2,1)S(1)}, bf16[256,256]{1,0:T(8,128)(2,1)S(1)}, u32[]{:S(2)}, u32[]{:S(2)}) %collective-permute-start.19) | collective-permute-done | bytes 131104 | tf_op jit(solution)/shard_map/ppermute | solution.py:24
  61.4 0.1 pad_maximum_fusion.1
  61.5 1.4 %collective-permute-start.23 = (bf16[256,256]{1,0:T(8,128)(2,1)S(1)}, bf16[256,256]{1,0:T(8,128)(2,1)S(1)}, u32[]{:S(2)}, u32[]{:S(2)}) collective-permute-start(bf16[256,256]{1,0:T(8,128)(2,1)S(1)} %get-tuple-element.49), channel_id=1, source_target_pairs={{0,24},{8,16},{16,8},{24,0},{1,25},{9,17},{17,9},{25,1},{2,26},{10... | collective-permute-start | bytes 393224 | tf_op jit(solution)/shard_map/ppermute | solution.py:24
  63.0 1.5 %collective-permute-start.22 = (bf16[256,256]{1,0:T(8,128)(2,1)S(1)}, bf16[256,256]{1,0:T(8,128)(2,1)S(1)}, u32[]{:S(2)}, u32[]{:S(2)}) collective-permute-start(bf16[256,256]{1,0:T(8,128)(2,1)S(1)} %get-tuple-element.50), channel_id=1, source_target_pairs={{0,16},{8,24},{16,0},{24,8},{1,17},{9,25},{17,1},{25,9},{2,18},{10... | collective-permute-start | bytes 393224 | tf_op jit(solution)/shard_map/ppermute | solution.py:24
  64.5 0.6 collective-permute-start.21
  65.1 0.2 concatenate.3.refs_0_
  65.3 1.4 %collective-permute-start.14 = (bf16[528,256]{1,0:T(8,128)(2,1)S(1)}, bf16[528,256]{1,0:T(8,128)(2,1)S(1)}, u32[]{:S(2)}, u32[]{:S(2)}) collective-permute-start(bf16[528,256]{1,0:T(8,128)(2,1)S(1)} %concatenate.3.refs_0_), channel_id=1, source_target_pairs={{0,24},{8,16},{16,8},{24,0},{1,25},{9,17},{17,9},{25,1},{2,26},{10... | collective-permute-start | bytes 811016 | tf_op jit(solution)/shard_map/ppermute | solution.py:24
  66.7 1.5 %collective-permute-start.13 = (bf16[528,256]{1,0:T(8,128)(2,1)S(1)}, bf16[528,256]{1,0:T(8,128)(2,1)S(1)}, u32[]{:S(2)}, u32[]{:S(2)}) collective-permute-start(bf16[528,256]{1,0:T(8,128)(2,1)S(1)} %concatenate.3.refs_0_), channel_id=1, source_target_pairs={{0,16},{8,24},{16,0},{24,8},{1,17},{9,25},{17,1},{25,9},{2,18},{10... | collective-permute-start | bytes 811016 | tf_op jit(solution)/shard_map/ppermute | solution.py:24
  68.2 0.6 collective-permute-done.23.refs_3_
  68.9 7.4 %collective-permute-done.22.refs_2_ = bf16[256,256]{1,0:T(8,128)(2,1)S(1)} collective-permute-done((bf16[256,256]{1,0:T(8,128)(2,1)S(1)}, bf16[256,256]{1,0:T(8,128)(2,1)S(1)}, u32[]{:S(2)}, u32[]{:S(2)}) %collective-permute-start.22) | collective-permute-done | bytes 131104 | tf_op jit(solution)/shard_map/ppermute | solution.py:24
  76.3 0.0 collective-permute-done.21.refs_1_
  76.3 0.1 pad_maximum_fusion.2
  76.4 0.1 collective-permute-start.24
  76.4 1.4 %collective-permute-start.12 = (bf16[528,256]{1,0:T(8,128)(2,1)S(1)}, bf16[528,256]{1,0:T(8,128)(2,1)S(1)}, u32[]{:S(2)}, u32[]{:S(2)}) collective-permute-start(bf16[528,256]{1,0:T(8,128)(2,1)S(1)} %concatenate.3.refs_0_), channel_id=1, source_target_pairs={{0,8},{8,0},{16,24},{24,16},{1,9},{9,1},{17,25},{25,17},{2,10},{10... | collective-permute-start | bytes 811016 | tf_op jit(solution)/shard_map/ppermute | solution.py:24
  77.9 2.5 %collective-permute-start.5 = (bf16[256,256]{1,0:T(8,128)(2,1)S(1)}, bf16[256,256]{1,0:T(8,128)(2,1)S(1)}, u32[]{:S(2)}, u32[]{:S(2)}) collective-permute-start(bf16[256,256]{1,0:T(8,128)(2,1)S(1)} %get-tuple-element.33), channel_id=1, source_target_pairs={{0,6},{1,7},{2,4},{3,5},{4,2},{5,3},{6,0},{7,1},{8,14},{9,15},{10,... | collective-permute-start | bytes 393224 | tf_op jit(solution)/shard_map/ppermute | solution.py:24
  80.3 0.0 collective-permute-done.14.refs_3_
  80.3 1.6 %collective-permute-done.13.refs_2_ = bf16[528,256]{1,0:T(8,128)(2,1)S(1)} collective-permute-done((bf16[528,256]{1,0:T(8,128)(2,1)S(1)}, bf16[528,256]{1,0:T(8,128)(2,1)S(1)}, u32[]{:S(2)}, u32[]{:S(2)}) %collective-permute-start.13) | collective-permute-done | bytes 270368 | tf_op jit(solution)/shard_map/ppermute | solution.py:24
  81.9 0.3 collective-permute-start.3
  82.3 3.1 %collective-permute-done.12.refs_1_ = bf16[528,256]{1,0:T(8,128)(2,1)S(1)} collective-permute-done((bf16[528,256]{1,0:T(8,128)(2,1)S(1)}, bf16[528,256]{1,0:T(8,128)(2,1)S(1)}, u32[]{:S(2)}, u32[]{:S(2)}) %collective-permute-start.12) | collective-permute-done | bytes 270368 | tf_op jit(solution)/shard_map/ppermute | solution.py:24
  85.3 2.8 %shift.1.refs_5_ = bf16[8,1024,512]{2,1,0:T(8,128)(2,1)S(1)} custom-call(s32[8]{0:T(128)S(1)} %copy-done, bf16[528,256]{1,0:T(8,128)(2,1)S(1)} %concatenate.3.refs_0_, bf16[528,256]{1,0:T(8,128)(2,1)S(1)} %collective-permute-done.12.refs_1_, bf16[528,256]{1,0:T(8,128)(2,1)S(1)} %collective-permute-done.13.refs_2_, ...), custom_call_target="tpu_custom_call" | custom-call | bytes 9437184 | tf_op jit(solution)/shard_map/shift/pallas_call | solution.py:284
  88.2 0.0 collective-permute-done.5
  88.2 2.9 %collective-permute-done.4 = bf16[256,256]{1,0:T(8,128)(2,1)S(1)} collective-permute-done((bf16[256,256]{1,0:T(8,128)(2,1)S(1)}, bf16[256,256]{1,0:T(8,128)(2,1)S(1)}, u32[]{:S(2)}, u32[]{:S(2)}) %collective-permute-start.4) | collective-permute-done | bytes 131104 | tf_op jit(solution)/shard_map/ppermute | solution.py:24
  91.1 0.0 collective-permute-done.3
  91.1 0.1 pad_maximum_fusion
  91.3 0.8 collective-permute-start.17
  92.1 1.4 %collective-permute-start.16 = (bf16[256,256]{1,0:T(8,128)(2,1)S(1)}, bf16[256,256]{1,0:T(8,128)(2,1)S(1)}, u32[]{:S(2)}, u32[]{:S(2)}) collective-permute-start(bf16[256,256]{1,0:T(8,128)(2,1)S(1)} %get-tuple-element.54), channel_id=1, source_target_pairs={{0,16},{8,24},{16,0},{24,8},{1,17},{9,25},{17,1},{25,9},{2,18},{10... | collective-permute-start | bytes 393224 | tf_op jit(solution)/shard_map/ppermute | solution.py:24
  93.5 1.3 %collective-permute-start.15 = (bf16[256,256]{1,0:T(8,128)(2,1)S(1)}, bf16[256,256]{1,0:T(8,128)(2,1)S(1)}, u32[]{:S(2)}, u32[]{:S(2)}) collective-permute-start(bf16[256,256]{1,0:T(8,128)(2,1)S(1)} %get-tuple-element.55), channel_id=1, source_target_pairs={{0,8},{8,0},{16,24},{24,16},{1,9},{9,1},{17,25},{25,17},{2,10},{10... | collective-permute-start | bytes 393224 | tf_op jit(solution)/shard_map/ppermute | solution.py:24
  94.8 7.6 %correlate.2.refs_6_ = f32[8,1024,512]{2,1,0:T(8,128)} custom-call(f32[8]{0:T(128)S(1)} %convert_rsqrt_fusion.factors, bf16[256,256]{1,0:T(8,128)(2,1)S(1)} %bitcast.30, bf16[256,256]{1,0:T(8,128)(2,1)S(1)} %collective-permute-done.21.refs_1_, bf16[256,256]{1,0:T(8,128)(2,1)S(1)} %collective-permute-done.22.refs_2_, ...), custom_call_target="tpu_custom_call" | custom-call | flops 4294967296 | bytes 16777216 | tf_op jit(solution)/shard_map/correlate/pallas_call | solution.py:364
  102.5 0.0 collective-permute-done.16.refs_2_
  102.5 0.0 collective-permute-done.15.refs_1_
  102.5 0.1 pad_maximum_fusion.3
  102.6 0.1 collective-permute-start.25
  102.7 1.9 %collective-permute-done.25.refs_4_ = bf16[4,256,256]{2,1,0:T(8,128)(2,1)S(1)} collective-permute-done((bf16[4,256,256]{2,1,0:T(8,128)(2,1)S(1)}, bf16[4,256,256]{2,1,0:T(8,128)(2,1)S(1)}, u32[]{:S(2)}, u32[]{:S(2)}) %collective-permute-start.25) | collective-permute-done | bytes 524320 | tf_op jit(solution)/shard_map/ppermute | solution.py:24
  104.5 7.6 %correlate.3 = f32[8,1024,512]{2,1,0:T(8,128)} custom-call(f32[8]{0:T(128)S(1)} %convert_rsqrt_fusion.factors, bf16[256,256]{1,0:T(8,128)(2,1)S(1)} %get-tuple-element.37.refs_0_, bf16[256,256]{1,0:T(8,128)(2,1)S(1)} %collective-permute-done.15.refs_1_, bf16[256,256]{1,0:T(8,128)(2,1)S(1)} %collective-permute-done.16.refs_2_, ...), custom_call_target="tpu_custom_call", output_to_operand_aliasing={{}: (7, {})} | custom-call | flops 4294967296 | bytes 16777216 | tf_op jit(solution)/shard_map/correlate/pallas_call | solution.py:364
  (20 shorter events, 0.2 us)
Async XLA Ops:
  11.5 19.5 %collective-permute-start.1 = (f32[256,256]{1,0:T(8,128)S(1)}, f32[256,256]{1,0:T(8,128)S(1)}, u32[]{:S(2)}, u32[]{:S(2)}) collective-permute-start(f32[256,256]{1,0:T(8,128)S(1)} %get-tuple-element.28), channel_id=1, source_target_pairs={{0,16},{8,24},{16,0},{24,8},{1,17},{9,25},{17,1},{25,9},{2,18},{10... | collective-permute-start | bytes 786440 | tf_op jit(solution)/shard_map/ppermute | solution.py:24
  14.6 10.3 %collective-permute-start.7 = (f32[256,256]{1,0:T(8,128)S(1)}, f32[256,256]{1,0:T(8,128)S(1)}, u32[]{:S(2)}, u32[]{:S(2)}) collective-permute-start(f32[256,256]{1,0:T(8,128)S(1)} %get-tuple-element.32), channel_id=1, source_target_pairs={{0,8},{8,0},{16,24},{24,16},{1,9},{9,1},{17,25},{25,17},{2,10},{10... | collective-permute-start | bytes 786440 | tf_op jit(solution)/shard_map/ppermute | solution.py:24
  20.1 12.4 %collective-permute-start.6 = (f32[256,256]{1,0:T(8,128)S(1)}, f32[256,256]{1,0:T(8,128)S(1)}, u32[]{:S(2)}, u32[]{:S(2)}) collective-permute-start(f32[256,256]{1,0:T(8,128)S(1)} %get-tuple-element.30), channel_id=1, source_target_pairs={{0,8},{8,0},{16,24},{24,16},{1,9},{9,1},{17,25},{25,17},{2,10},{10... | collective-permute-start | bytes 786440 | tf_op jit(solution)/shard_map/ppermute | solution.py:24
  25.0 9.2 %collective-permute-start.8 = (f32[256,256]{1,0:T(8,128)S(1)}, f32[256,256]{1,0:T(8,128)S(1)}, u32[]{:S(2)}, u32[]{:S(2)}) collective-permute-start(f32[256,256]{1,0:T(8,128)S(1)} %add.58), channel_id=1, source_target_pairs={{0,16},{8,24},{16,0},{24,8},{1,17},{9,25},{17,1},{25,9},{2,18},{10... | collective-permute-start | bytes 786440 | tf_op jit(solution)/shard_map/ppermute | solution.py:24
  25.1 57.2 %copy-start = (s32[8]{0:T(128)S(1)}, s32[8]{0:T(128)}, u32[]{:S(2)}) copy-start(s32[8]{0:T(128)} %offsets.1) | copy-start | bytes 100
  25.1 12.7 %collective-permute-start = (f32[256,256]{1,0:T(8,128)S(1)}, f32[256,256]{1,0:T(8,128)S(1)}, u32[]{:S(2)}, u32[]{:S(2)}) collective-permute-start(f32[256,256]{1,0:T(8,128)S(1)} %get-tuple-element.26), channel_id=1, source_target_pairs={{0,16},{8,24},{16,0},{24,8},{1,17},{9,25},{17,1},{25,9},{2,18},{10... | collective-permute-start | bytes 786440 | tf_op jit(solution)/shard_map/ppermute | solution.py:24
  31.0 6.9 %collective-permute-start.2 = (f32[256,256]{1,0:T(8,128)S(1)}, f32[256,256]{1,0:T(8,128)S(1)}, u32[]{:S(2)}, u32[]{:S(2)}) collective-permute-start(f32[256,256]{1,0:T(8,128)S(1)} %add.55), channel_id=1, source_target_pairs={{0,8},{8,0},{16,24},{24,16},{1,9},{9,1},{17,25},{25,17},{2,10},{10... | collective-permute-start | bytes 786440 | tf_op jit(solution)/shard_map/ppermute | solution.py:24
  37.9 3.6 %collective-permute-start.9 = (f32[256]{0:T(256)S(1)}, f32[256]{0:T(256)S(1)}, u32[]{:S(2)}, u32[]{:S(2)}) collective-permute-start(f32[256]{0:T(256)S(1)} %add.60), channel_id=1, source_target_pairs={{0,2},{1,3},{2,0},{3,1},{4,6},{5,7},{6,4},{7,5},{8,10},{9,11},{10,... | collective-permute-start | bytes 3080 | tf_op jit(solution)/shard_map/ppermute | solution.py:24
  41.6 4.5 %collective-permute-start.10 = (f32[256]{0:T(256)S(1)}, f32[256]{0:T(256)S(1)}, u32[]{:S(2)}, u32[]{:S(2)}) collective-permute-start(f32[256]{0:T(256)S(1)} %add.61), channel_id=1, source_target_pairs={{0,4},{1,5},{2,6},{3,7},{4,0},{5,1},{6,2},{7,3},{8,12},{9,13},{10,... | collective-permute-start | bytes 3080 | tf_op jit(solution)/shard_map/ppermute | solution.py:24
  46.1 4.4 %collective-permute-start.11 = (f32[256]{0:T(256)S(1)}, f32[256]{0:T(256)S(1)}, u32[]{:S(2)}, u32[]{:S(2)}) collective-permute-start(f32[256]{0:T(256)S(1)} %add.62), channel_id=1, source_target_pairs={{0,1},{1,0},{2,3},{3,2},{4,5},{5,4},{6,7},{7,6},{8,9},{9,8},{10,11... | collective-permute-start | bytes 3080 | tf_op jit(solution)/shard_map/ppermute | solution.py:24
  46.1 8.3 %collective-permute-start.20 = (bf16[256,256]{1,0:T(8,128)(2,1)S(1)}, bf16[256,256]{1,0:T(8,128)(2,1)S(1)}, u32[]{:S(2)}, u32[]{:S(2)}) collective-permute-start(bf16[256,256]{1,0:T(8,128)(2,1)S(1)} %get-tuple-element.43), channel_id=1, source_target_pairs={{0,6},{1,7},{2,4},{3,5},{4,2},{5,3},{6,0},{7,1},{8,14},{9,15},{10,... | collective-permute-start | bytes 393224 | tf_op jit(solution)/shard_map/ppermute | solution.py:24
  49.7 11.7 %collective-permute-start.19 = (bf16[256,256]{1,0:T(8,128)(2,1)S(1)}, bf16[256,256]{1,0:T(8,128)(2,1)S(1)}, u32[]{:S(2)}, u32[]{:S(2)}) collective-permute-start(bf16[256,256]{1,0:T(8,128)(2,1)S(1)} %get-tuple-element.43), channel_id=1, source_target_pairs={{0,4},{1,5},{2,6},{3,7},{4,0},{5,1},{6,2},{7,3},{8,12},{9,13},{10,... | collective-permute-start | bytes 393224 | tf_op jit(solution)/shard_map/ppermute | solution.py:24
  49.7 11.7 %collective-permute-start.18 = (bf16[256,256]{1,0:T(8,128)(2,1)S(1)}, bf16[256,256]{1,0:T(8,128)(2,1)S(1)}, u32[]{:S(2)}, u32[]{:S(2)}) collective-permute-start(bf16[256,256]{1,0:T(8,128)(2,1)S(1)} %get-tuple-element.43), channel_id=1, source_target_pairs={{0,2},{1,3},{2,0},{3,1},{4,6},{5,7},{6,4},{7,5},{8,10},{9,11},{10,... | collective-permute-start | bytes 393224 | tf_op jit(solution)/shard_map/ppermute | solution.py:24
  61.5 7.3 %collective-permute-start.23 = (bf16[256,256]{1,0:T(8,128)(2,1)S(1)}, bf16[256,256]{1,0:T(8,128)(2,1)S(1)}, u32[]{:S(2)}, u32[]{:S(2)}) collective-permute-start(bf16[256,256]{1,0:T(8,128)(2,1)S(1)} %get-tuple-element.49), channel_id=1, source_target_pairs={{0,24},{8,16},{16,8},{24,0},{1,25},{9,17},{17,9},{25,1},{2,26},{10... | collective-permute-start | bytes 393224 | tf_op jit(solution)/shard_map/ppermute | solution.py:24
  63.0 13.3 %collective-permute-start.22 = (bf16[256,256]{1,0:T(8,128)(2,1)S(1)}, bf16[256,256]{1,0:T(8,128)(2,1)S(1)}, u32[]{:S(2)}, u32[]{:S(2)}) collective-permute-start(bf16[256,256]{1,0:T(8,128)(2,1)S(1)} %get-tuple-element.50), channel_id=1, source_target_pairs={{0,16},{8,24},{16,0},{24,8},{1,17},{9,25},{17,1},{25,9},{2,18},{10... | collective-permute-start | bytes 393224 | tf_op jit(solution)/shard_map/ppermute | solution.py:24
  64.5 11.8 %collective-permute-start.21 = (bf16[256,256]{1,0:T(8,128)(2,1)S(1)}, bf16[256,256]{1,0:T(8,128)(2,1)S(1)}, u32[]{:S(2)}, u32[]{:S(2)}) collective-permute-start(bf16[256,256]{1,0:T(8,128)(2,1)S(1)} %get-tuple-element.51), channel_id=1, source_target_pairs={{0,8},{8,0},{16,24},{24,16},{1,9},{9,1},{17,25},{25,17},{2,10},{10... | collective-permute-start | bytes 393224 | tf_op jit(solution)/shard_map/ppermute | solution.py:24
  65.3 15.0 %collective-permute-start.14 = (bf16[528,256]{1,0:T(8,128)(2,1)S(1)}, bf16[528,256]{1,0:T(8,128)(2,1)S(1)}, u32[]{:S(2)}, u32[]{:S(2)}) collective-permute-start(bf16[528,256]{1,0:T(8,128)(2,1)S(1)} %concatenate.3.refs_0_), channel_id=1, source_target_pairs={{0,24},{8,16},{16,8},{24,0},{1,25},{9,17},{17,9},{25,1},{2,26},{10... | collective-permute-start | bytes 811016 | tf_op jit(solution)/shard_map/ppermute | solution.py:24
  66.7 15.2 %collective-permute-start.13 = (bf16[528,256]{1,0:T(8,128)(2,1)S(1)}, bf16[528,256]{1,0:T(8,128)(2,1)S(1)}, u32[]{:S(2)}, u32[]{:S(2)}) collective-permute-start(bf16[528,256]{1,0:T(8,128)(2,1)S(1)} %concatenate.3.refs_0_), channel_id=1, source_target_pairs={{0,16},{8,24},{16,0},{24,8},{1,17},{9,25},{17,1},{25,9},{2,18},{10... | collective-permute-start | bytes 811016 | tf_op jit(solution)/shard_map/ppermute | solution.py:24
  76.4 18.5 %collective-permute-start.24 = (bf16[4,256,256]{2,1,0:T(8,128)(2,1)S(1)}, bf16[4,256,256]{2,1,0:T(8,128)(2,1)S(1)}, u32[]{:S(2)}, u32[]{:S(2)}) collective-permute-start(bf16[4,256,256]{2,1,0:T(8,128)(2,1)S(1)} %pad_maximum_fusion.2), channel_id=1, source_target_pairs={{0,1},{1,0},{2,3},{3,2},{4,5},{5,4},{6,7},{7,6},{8,9},{9,8},{10,11... | collective-permute-start | bytes 1572872 | tf_op jit(solution)/shard_map/ppermute | solution.py:24
  76.4 8.9 %collective-permute-start.12 = (bf16[528,256]{1,0:T(8,128)(2,1)S(1)}, bf16[528,256]{1,0:T(8,128)(2,1)S(1)}, u32[]{:S(2)}, u32[]{:S(2)}) collective-permute-start(bf16[528,256]{1,0:T(8,128)(2,1)S(1)} %concatenate.3.refs_0_), channel_id=1, source_target_pairs={{0,8},{8,0},{16,24},{24,16},{1,9},{9,1},{17,25},{25,17},{2,10},{10... | collective-permute-start | bytes 811016 | tf_op jit(solution)/shard_map/ppermute | solution.py:24
  77.9 10.3 %collective-permute-start.5 = (bf16[256,256]{1,0:T(8,128)(2,1)S(1)}, bf16[256,256]{1,0:T(8,128)(2,1)S(1)}, u32[]{:S(2)}, u32[]{:S(2)}) collective-permute-start(bf16[256,256]{1,0:T(8,128)(2,1)S(1)} %get-tuple-element.33), channel_id=1, source_target_pairs={{0,6},{1,7},{2,4},{3,5},{4,2},{5,3},{6,0},{7,1},{8,14},{9,15},{10,... | collective-permute-start | bytes 393224 | tf_op jit(solution)/shard_map/ppermute | solution.py:24
  80.3 10.8 %collective-permute-start.4 = (bf16[256,256]{1,0:T(8,128)(2,1)S(1)}, bf16[256,256]{1,0:T(8,128)(2,1)S(1)}, u32[]{:S(2)}, u32[]{:S(2)}) collective-permute-start(bf16[256,256]{1,0:T(8,128)(2,1)S(1)} %get-tuple-element.33), channel_id=1, source_target_pairs={{0,4},{1,5},{2,6},{3,7},{4,0},{5,1},{6,2},{7,3},{8,12},{9,13},{10,... | collective-permute-start | bytes 393224 | tf_op jit(solution)/shard_map/ppermute | solution.py:24
  81.9 9.2 %collective-permute-start.3 = (bf16[256,256]{1,0:T(8,128)(2,1)S(1)}, bf16[256,256]{1,0:T(8,128)(2,1)S(1)}, u32[]{:S(2)}, u32[]{:S(2)}) collective-permute-start(bf16[256,256]{1,0:T(8,128)(2,1)S(1)} %get-tuple-element.33), channel_id=1, source_target_pairs={{0,2},{1,3},{2,0},{3,1},{4,6},{5,7},{6,4},{7,5},{8,10},{9,11},{10,... | collective-permute-start | bytes 393224 | tf_op jit(solution)/shard_map/ppermute | solution.py:24
  91.3 11.2 %collective-permute-start.17 = (bf16[256,256]{1,0:T(8,128)(2,1)S(1)}, bf16[256,256]{1,0:T(8,128)(2,1)S(1)}, u32[]{:S(2)}, u32[]{:S(2)}) collective-permute-start(bf16[256,256]{1,0:T(8,128)(2,1)S(1)} %get-tuple-element.53), channel_id=1, source_target_pairs={{0,24},{8,16},{16,8},{24,0},{1,25},{9,17},{17,9},{25,1},{2,26},{10... | collective-permute-start | bytes 393224 | tf_op jit(solution)/shard_map/ppermute | solution.py:24
  92.1 10.4 %collective-permute-start.16 = (bf16[256,256]{1,0:T(8,128)(2,1)S(1)}, bf16[256,256]{1,0:T(8,128)(2,1)S(1)}, u32[]{:S(2)}, u32[]{:S(2)}) collective-permute-start(bf16[256,256]{1,0:T(8,128)(2,1)S(1)} %get-tuple-element.54), channel_id=1, source_target_pairs={{0,16},{8,24},{16,0},{24,8},{1,17},{9,25},{17,1},{25,9},{2,18},{10... | collective-permute-start | bytes 393224 | tf_op jit(solution)/shard_map/ppermute | solution.py:24
  93.5 9.0 %collective-permute-start.15 = (bf16[256,256]{1,0:T(8,128)(2,1)S(1)}, bf16[256,256]{1,0:T(8,128)(2,1)S(1)}, u32[]{:S(2)}, u32[]{:S(2)}) collective-permute-start(bf16[256,256]{1,0:T(8,128)(2,1)S(1)} %get-tuple-element.55), channel_id=1, source_target_pairs={{0,8},{8,0},{16,24},{24,16},{1,9},{9,1},{17,25},{25,17},{2,10},{10... | collective-permute-start | bytes 393224 | tf_op jit(solution)/shard_map/ppermute | solution.py:24
  102.6 2.0 %collective-permute-start.25 = (bf16[4,256,256]{2,1,0:T(8,128)(2,1)S(1)}, bf16[4,256,256]{2,1,0:T(8,128)(2,1)S(1)}, u32[]{:S(2)}, u32[]{:S(2)}) collective-permute-start(bf16[4,256,256]{2,1,0:T(8,128)(2,1)S(1)} %pad_maximum_fusion.3), channel_id=1, source_target_pairs={{0,1},{1,0},{2,3},{3,2},{4,5},{5,4},{6,7},{7,6},{8,9},{9,8},{10,11... | collective-permute-start | bytes 1572872 | tf_op jit(solution)/shard_map/ppermute | solution.py:24
